TPU v7x, 32 devices: a whole 2x2x4 slice. The times are simulated.
32 devices in a mesh: dp: 32 (over z, y, x, core).
Axes of the slice: x: 2, y: 2, z: 4, core: 2. Of those that a mesh axis runs over, the one named last changes fastest.
Arguments:
- tokens: bfloat16 [192, 2, 197, 384], P('dp'), may hold values from -60 to 60
- counts: int32 [192], P('dp'), may hold values from 1 to 2, as said below
- cotangent: float32 [192, 2, 197, 384], P('dp'), may hold values from -6 to 6
- norm_gain: float32 [2, 2, 384], P(None, None, 'dp'), may hold values from 0.5 to 1.5
- bias_rows: float32 [2, 6, 384], P(None, None, 'dp'), may hold values from -1.8 to 1.8
- up_bias: float32 [2, 1536], P(None, 'dp'), may hold values from -1.8 to 1.8
- qkv_weight: float32 [2, 384, 1152], P(None, 'dp'), may hold values from -12 to 12
- out_weight: float32 [2, 384, 384], P(None, 'dp'), may hold values from -1.25 to 1.25
- up_weight: float32 [2, 384, 1536], P(None, 'dp'), may hold values from -0.3125 to 0.3125
- down_weight: float32 [2, 1536, 384], P(None, 'dp'), may hold values from -0.15625 to 0.15625
- first_norm_gain: float32 [2, 2, 384], P(None, None, 'dp'), may hold values from -0.06 to 0.06
- first_bias_rows: float32 [2, 6, 384], P(None, None, 'dp'), may hold values from -0.06 to 0.06
- first_up_bias: float32 [2, 1536], P(None, 'dp'), may hold values from -0.06 to 0.06
- first_qkv_weight: float32 [2, 384, 1152], P(None, 'dp'), may hold values from -0.06 to 0.06
- first_out_weight: float32 [2, 384, 384], P(None, 'dp'), may hold values from -0.06 to 0.06
- first_up_weight: float32 [2, 384, 1536], P(None, 'dp'), may hold values from -0.06 to 0.06
- first_down_weight: float32 [2, 1536, 384], P(None, 'dp'), may hold values from -0.06 to 0.06
- second_norm_gain: float32 [2, 2, 384], P(None, None, 'dp'), may hold values from 1e-05 to 0.001
- second_bias_rows: float32 [2, 6, 384], P(None, None, 'dp'), may hold values from 1e-05 to 0.001
- second_up_bias: float32 [2, 1536], P(None, 'dp'), may hold values from 1e-05 to 0.001
- second_qkv_weight: float32 [2, 384, 1152], P(None, 'dp'), may hold values from 1e-05 to 0.001
- second_out_weight: float32 [2, 384, 384], P(None, 'dp'), may hold values from 1e-05 to 0.001
- second_up_weight: float32 [2, 384, 1536], P(None, 'dp'), may hold values from 1e-05 to 0.001
- second_down_weight: float32 [2, 1536, 384], P(None, 'dp'), may hold values from 1e-05 to 0.001
Outputs:
- block_out: float32 [192, 2, 197, 384], P('dp')
- input_grad: float32 [192, 2, 197, 384], P('dp')
- grad_norm_gain: float32 [2, 2, 384], P(None, None, 'dp')
- grad_bias_rows: float32 [2, 6, 384], P(None, None, 'dp')
- grad_up_bias: float32 [2, 1536], P(None, 'dp')
- grad_qkv_weight: float32 [2, 384, 1152], P(None, 'dp')
- grad_out_weight: float32 [2, 384, 384], P(None, 'dp')
- grad_up_weight: float32 [2, 384, 1536], P(None, 'dp')
- grad_down_weight: float32 [2, 1536, 384], P(None, 'dp')
- new_norm_gain: float32 [2, 2, 384], P(None, None, 'dp')
- new_bias_rows: float32 [2, 6, 384], P(None, None, 'dp')
- new_up_bias: float32 [2, 1536], P(None, 'dp')
- new_qkv_weight: float32 [2, 384, 1152], P(None, 'dp')
- new_out_weight: float32 [2, 384, 384], P(None, 'dp')
- new_up_weight: float32 [2, 384, 1536], P(None, 'dp')
- new_down_weight: float32 [2, 1536, 384], P(None, 'dp')
- new_first_norm_gain: float32 [2, 2, 384], P(None, None, 'dp')
- new_first_bias_rows: float32 [2, 6, 384], P(None, None, 'dp')
- new_first_up_bias: float32 [2, 1536], P(None, 'dp')
- new_first_qkv_weight: float32 [2, 384, 1152], P(None, 'dp')
- new_first_out_weight: float32 [2, 384, 384], P(None, 'dp')
- new_first_up_weight: float32 [2, 384, 1536], P(None, 'dp')
- new_first_down_weight: float32 [2, 1536, 384], P(None, 'dp')
- new_second_norm_gain: float32 [2, 2, 384], P(None, None, 'dp')
- new_second_bias_rows: float32 [2, 6, 384], P(None, None, 'dp')
- new_second_up_bias: float32 [2, 1536], P(None, 'dp')
- new_second_qkv_weight: float32 [2, 384, 1152], P(None, 'dp')
- new_second_out_weight: float32 [2, 384, 384], P(None, 'dp')
- new_second_up_weight: float32 [2, 384, 1536], P(None, 'dp')
- new_second_down_weight: float32 [2, 1536, 384], P(None, 'dp')
Inputs may be any that keep to these rules, and one draw needn't show every extreme that they name: counts[g] images fill group g: slot 0 always, slot 1 only when counts[g] is 2; every draw has groups of both kinds.
All inputs are finite; a program needn't handle non-finite values.
Results may differ from a plain program's by a relative error of at most 0.02.
The roundings to bfloat16 on the way count: a program that leaves them out, or rounds other values in their place, can miss the bound.
Values may be sent and summed in bfloat16 or wider, within the bound.
No kernel may reach another device: no remote copies, remote signals or barrier semaphores. Data moves between devices by JAX's collectives and lax.ppermute only.
A program may use at most 320 MiB of HBM per device.

v0:
```python
import jax
import jax.numpy as jnp
from jax import lax
from jax.sharding import PartitionSpec as P

HD = 64
STEP = 3


BETA_ONE = 0.9
BETA_TWO = 0.95
LEARN_RATE = 0.02
DECAY = 0.05
ADAM_EPS = 1e-08
NORM_EPS = 1e-06


def mixed(form, left, right):
    return jnp.einsum(form, left, right, preferred_element_type=jnp.float32)


def cross_rows(left, right):
    return lax.dot_general(
        left, right, (((0,), (0,)), ((), ())), preferred_element_type=jnp.float32
    )


def back_dot(left, weight):
    return lax.dot_general(
        left, weight, (((1,), (1,)), ((), ())), preferred_element_type=jnp.float32
    )


def normalize(rows, gain, shift):
    center = rows - jnp.mean(rows, axis=-1, keepdims=True)
    rstd = lax.rsqrt(jnp.mean(center * center, axis=-1, keepdims=True) + NORM_EPS)
    normed = center * rstd
    return (normed * gain + shift, normed, rstd)


def norm_back(grad_in, gain, normed, rstd):
    scaled = grad_in * gain
    return rstd * (
        scaled
        - jnp.mean(scaled, axis=-1, keepdims=True)
        - normed * jnp.mean(scaled * normed, axis=-1, keepdims=True)
    )


def gelu_value(pre_act):
    return 0.5 * pre_act * (1.0 + lax.erf(pre_act * 0.7071067811865476))


def gelu_slope(pre_act):
    return (
        0.5 * (1.0 + lax.erf(pre_act * 0.7071067811865476))
        + pre_act * jnp.exp(-0.5 * pre_act * pre_act) * 0.3989422804014327
    )


def forward_layer(resid, weights, images, seq_len, head_size):
    gain_rows, shift_rows, up_shift, qkv_w, out_w, up_w, down_w = weights
    width = resid.shape[1]
    heads = width // head_size
    scale = head_size ** (-0.5)
    gains = gain_rows.astype(jnp.float32)
    shifts = shift_rows.astype(jnp.float32)
    first_f, normed_one, rstd_one = normalize(resid, gains[0], shifts[0])
    first_in = first_f.astype(jnp.bfloat16)
    proj = jnp.dot(first_in, qkv_w, preferred_element_type=jnp.float32)
    query = (
        ((proj[:, :width] + shifts[1]) * scale)
        .astype(jnp.bfloat16)
        .reshape(images, seq_len, heads, head_size)
    )
    keys = (
        proj[:, width : 2 * width].astype(jnp.bfloat16).reshape(images, seq_len, heads, head_size)
    )
    values = (
        (proj[:, 2 * width :] + shifts[2])
        .astype(jnp.bfloat16)
        .reshape(images, seq_len, heads, head_size)
    )
    scores = mixed("nqhd,nkhd->nhqk", query, keys)
    top = jnp.max(scores, axis=-1, keepdims=True)
    expo = jnp.exp(scores - top)
    total = jnp.sum(expo, axis=-1, keepdims=True)
    logsum = top + jnp.log(total)
    probs = (expo / total).astype(jnp.bfloat16)
    context = mixed("nhqk,nkhd->nqhd", probs, values).reshape(-1, width).astype(jnp.bfloat16)
    hidden_res = resid + jnp.dot(context, out_w, preferred_element_type=jnp.float32) + shifts[3]
    second_f, normed_two, rstd_two = normalize(hidden_res, gains[1], shifts[4])
    second_in = second_f.astype(jnp.bfloat16)
    pre_act = jnp.dot(second_in, up_w, preferred_element_type=jnp.float32) + up_shift.astype(
        jnp.float32
    )
    activ = gelu_value(pre_act).astype(jnp.bfloat16)
    result = hidden_res + jnp.dot(activ, down_w, preferred_element_type=jnp.float32) + shifts[5]
    saved = (
        first_in,
        normed_one,
        rstd_one,
        query,
        keys,
        values,
        logsum,
        context,
        normed_two,
        rstd_two,
        second_in,
        pre_act,
        activ,
    )
    return (result, saved)


def backward_layer(grad_out, weights, saved, head_size):
    gain_rows, shift_rows, up_shift, qkv_w, out_w, up_w, down_w = weights
    (
        first_in,
        normed_one,
        rstd_one,
        query,
        keys,
        values,
        logsum,
        context,
        normed_two,
        rstd_two,
        second_in,
        pre_act,
        activ,
    ) = saved
    width = grad_out.shape[1]
    scale = head_size ** (-0.5)
    gains = gain_rows.astype(jnp.float32)
    grad_low = grad_out.astype(jnp.bfloat16)
    grad_down = cross_rows(activ, grad_low)
    shift_five = jnp.sum(grad_out, axis=0)
    dpre = back_dot(grad_low, down_w) * gelu_slope(pre_act)
    dpre_low = dpre.astype(jnp.bfloat16)
    grad_up = cross_rows(second_in, dpre_low)
    grad_upshift = jnp.sum(dpre, axis=0)
    dsecond = back_dot(dpre_low, up_w)
    gain_two = jnp.sum(dsecond * normed_two, axis=0)
    shift_four = jnp.sum(dsecond, axis=0)
    dres = grad_out + norm_back(dsecond, gains[1], normed_two, rstd_two)
    dres_low = dres.astype(jnp.bfloat16)
    grad_outw = cross_rows(context, dres_low)
    shift_three = jnp.sum(dres, axis=0)
    dctx = back_dot(dres_low, out_w).astype(jnp.bfloat16).reshape(query.shape)
    scores = mixed("nqhd,nkhd->nhqk", query, keys)
    probs = jnp.exp(scores - logsum)
    probs_low = probs.astype(jnp.bfloat16)
    dvals = mixed("nhqk,nqhd->nkhd", probs_low, dctx).reshape(-1, width)
    dprobs = mixed("nqhd,nkhd->nhqk", dctx, values)
    inner = jnp.sum(probs * dprobs, axis=-1, keepdims=True)
    dscore = (probs * (dprobs - inner)).astype(jnp.bfloat16)
    dquery = (mixed("nhqk,nkhd->nqhd", dscore, keys) * scale).reshape(-1, width)
    dkeys = mixed("nhqk,nqhd->nkhd", dscore, query).reshape(-1, width)
    shift_one = jnp.sum(dquery, axis=0)
    shift_two = jnp.sum(dvals, axis=0)
    dproj = jnp.concatenate([dquery, dkeys, dvals], axis=1).astype(jnp.bfloat16)
    grad_qkv = cross_rows(first_in, dproj)
    dfirst = back_dot(dproj, qkv_w)
    gain_one = jnp.sum(dfirst * normed_one, axis=0)
    shift_zero = jnp.sum(dfirst, axis=0)
    dinput = dres + norm_back(dfirst, gains[0], normed_one, rstd_one)
    grads = (
        jnp.stack([gain_one, gain_two]),
        jnp.stack([shift_zero, shift_one, shift_two, shift_three, shift_four, shift_five]),
        grad_upshift,
        grad_qkv,
        grad_outw,
        grad_up,
        grad_down,
    )
    return (dinput, grads)


def adam_update(grad_sum, weight, first, second, count_rows, decay_on):
    grad = grad_sum / count_rows
    first_new = BETA_ONE * first + (1.0 - BETA_ONE) * grad
    second_new = BETA_TWO * second + (1.0 - BETA_TWO) * grad * grad
    fix_one = 1.0 - BETA_ONE**STEP
    fix_two = 1.0 - BETA_TWO**STEP
    direction = first_new / fix_one / (jnp.sqrt(second_new / fix_two) + ADAM_EPS)
    if decay_on:
        direction = direction + DECAY * weight
    return (grad, weight - LEARN_RATE * direction, first_new, second_new)


def layer_slice(params, layer):
    return tuple((p[layer].astype(jnp.bfloat16) for p in params))


def fetch_layer(params, layer):
    gain_part, shift_part, upshift_part, qkv_part, outw_part, up_part, down_part = layer_slice(
        params, layer
    )
    return (
        lax.all_gather(gain_part, "dp", axis=1, tiled=True),
        lax.all_gather(shift_part, "dp", axis=1, tiled=True),
        lax.all_gather(upshift_part, "dp", axis=0, tiled=True),
        lax.all_gather(qkv_part, "dp", axis=0, tiled=True),
        lax.all_gather(outw_part, "dp", axis=0, tiled=True),
        lax.all_gather(up_part, "dp", axis=0, tiled=True),
        lax.all_gather(down_part, "dp", axis=0, tiled=True),
    )


def fetch_again(params, layer):
    gain_part, shift_part, upshift_part, qkv_part, outw_part, up_part, down_part = layer_slice(
        params, layer
    )
    return (
        lax.all_gather(gain_part, "dp", axis=1, tiled=True),
        lax.all_gather(shift_part, "dp", axis=1, tiled=True),
        lax.all_gather(upshift_part, "dp", axis=0, tiled=True),
        lax.all_gather(qkv_part, "dp", axis=0, tiled=True),
        lax.all_gather(outw_part, "dp", axis=0, tiled=True),
        lax.all_gather(up_part, "dp", axis=0, tiled=True),
        lax.all_gather(down_part, "dp", axis=0, tiled=True),
    )


def reduce_layer(grads):
    gain_term, shift_term, upshift_term, qkv_term, outw_term, up_term, down_term = grads
    return (
        lax.psum_scatter(gain_term, "dp", scatter_dimension=1, tiled=True),
        lax.psum_scatter(shift_term, "dp", scatter_dimension=1, tiled=True),
        lax.psum_scatter(upshift_term, "dp", scatter_dimension=0, tiled=True),
        lax.psum_scatter(qkv_term, "dp", scatter_dimension=0, tiled=True),
        lax.psum_scatter(outw_term, "dp", scatter_dimension=0, tiled=True),
        lax.psum_scatter(up_term, "dp", scatter_dimension=0, tiled=True),
        lax.psum_scatter(down_term, "dp", scatter_dimension=0, tiled=True),
    )


def body(
    tokens,
    counts,
    cotangent,
    norm_gain,
    bias_rows,
    up_bias,
    qkv_weight,
    out_weight,
    up_weight,
    down_weight,
    first_norm_gain,
    first_bias_rows,
    first_up_bias,
    first_qkv_weight,
    first_out_weight,
    first_up_weight,
    first_down_weight,
    second_norm_gain,
    second_bias_rows,
    second_up_bias,
    second_qkv_weight,
    second_out_weight,
    second_up_weight,
    second_down_weight,
):
    params = (norm_gain, bias_rows, up_bias, qkv_weight, out_weight, up_weight, down_weight)
    firsts = (
        first_norm_gain,
        first_bias_rows,
        first_up_bias,
        first_qkv_weight,
        first_out_weight,
        first_up_weight,
        first_down_weight,
    )
    seconds = (
        second_norm_gain,
        second_bias_rows,
        second_up_bias,
        second_qkv_weight,
        second_out_weight,
        second_up_weight,
        second_down_weight,
    )
    groups = tokens.shape[0]
    seq_len = tokens.shape[2]
    width = tokens.shape[3]
    images = 2 * groups
    layers = qkv_weight.shape[0]
    live = jnp.stack([jnp.ones_like(counts), (counts == 2).astype(jnp.int32)], axis=1).astype(
        jnp.float32
    )
    live_rows = jnp.broadcast_to(live[:, :, None], (groups, 2, seq_len)).reshape(-1, 1)
    resid = tokens.astype(jnp.float32).reshape(-1, width)
    kept = []
    saved_all = []
    for layer in range(layers):
        gathered = fetch_layer(params, layer)
        kept.append(gathered)
        resid, saved = forward_layer(resid, gathered, images, seq_len, HD)
        saved_all.append(saved)
    block_out = (resid * live_rows).reshape(tokens.shape)
    grad = cotangent.reshape(-1, width) * live_rows
    reduced = [None] * layers
    for layer in reversed(range(layers)):
        weights = fetch_again(params, layer)
        grad, local = backward_layer(grad, weights, saved_all[layer], HD)
        reduced[layer] = reduce_layer(local)
    sums = tuple((jnp.stack([reduced[layer][i] for layer in range(layers)]) for i in range(7)))
    input_grad = (grad * live_rows).reshape(tokens.shape)
    count_rows = float(lax.axis_size("dp") * groups * 2 * seq_len)
    results = [
        adam_update(sums[i], params[i], firsts[i], seconds[i], count_rows, i >= 3) for i in range(7)
    ]
    return (
        block_out,
        input_grad,
        results[0][0],
        results[1][0],
        results[2][0],
        results[3][0],
        results[4][0],
        results[5][0],
        results[6][0],
        results[0][1],
        results[1][1],
        results[2][1],
        results[3][1],
        results[4][1],
        results[5][1],
        results[6][1],
        results[0][2],
        results[1][2],
        results[2][2],
        results[3][2],
        results[4][2],
        results[5][2],
        results[6][2],
        results[0][3],
        results[1][3],
        results[2][3],
        results[3][3],
        results[4][3],
        results[5][3],
        results[6][3],
    )


def solution(mesh):
    return jax.shard_map(
        body,
        mesh=mesh,
        in_specs=(
            P("dp", None, None, None),
            P("dp"),
            P("dp", None, None, None),
            P(None, None, "dp"),
            P(None, None, "dp"),
            P(None, "dp"),
            P(None, "dp", None),
            P(None, "dp", None),
            P(None, "dp", None),
            P(None, "dp", None),
            P(None, None, "dp"),
            P(None, None, "dp"),
            P(None, "dp"),
            P(None, "dp", None),
            P(None, "dp", None),
            P(None, "dp", None),
            P(None, "dp", None),
            P(None, None, "dp"),
            P(None, None, "dp"),
            P(None, "dp"),
            P(None, "dp", None),
            P(None, "dp", None),
            P(None, "dp", None),
            P(None, "dp", None),
        ),
        out_specs=(
            P("dp", None, None, None),
            P("dp", None, None, None),
            P(None, None, "dp"),
            P(None, None, "dp"),
            P(None, "dp"),
            P(None, "dp", None),
            P(None, "dp", None),
            P(None, "dp", None),
            P(None, "dp", None),
            P(None, None, "dp"),
            P(None, None, "dp"),
            P(None, "dp"),
            P(None, "dp", None),
            P(None, "dp", None),
            P(None, "dp", None),
            P(None, "dp", None),
            P(None, None, "dp"),
            P(None, None, "dp"),
            P(None, "dp"),
            P(None, "dp", None),
            P(None, "dp", None),
            P(None, "dp", None),
            P(None, "dp", None),
            P(None, None, "dp"),
            P(None, None, "dp"),
            P(None, "dp"),
            P(None, "dp", None),
            P(None, "dp", None),
            P(None, "dp", None),
            P(None, "dp", None),
        ),
        check_vma=False,
    )
```

profile of v0, /device:TPU:0, one launch (start us, length us, event | category | flops | bytes accessed | tf_op | source)
XLA Modules:
  0.0 1307.0 jit_solution(14078467237861299334)
XLA Ops:
  15.5 16.8 %multiply_reduce_fusion.14 = f32[6,2,197]{1,2,0:T(8,128)S(1)} fusion(f32[6,2,197]{1,2,0:T(8,128)S(1)} %broadcast_multiply_fusion, bf16[6,2,197,384]{3,1,2,0:T(2,128)(2,1)S(1)} %copy-done.20), kind=kLoop, calls=%fused_computation.98 | loop fusion | flops 3628740 | bytes 1834464 | tf_op jit(solution)/shard_map/reduce_sum | solution.py:36
  42.4 42.7 %all-reduce.22 = (bf16[1536]{0:T(1024)(128)(2,1)S(1)}, bf16[1536]{0:T(1024)(128)(2,1)S(1)}) all-reduce(bf16[1536]{0:T(1024)(128)(2,1)S(1)} %dynamic-update-slice, bf16[1536]{0:T(1024)(128)(2,1)S(1)} %dynamic-update-slice.1), channel_id=7, replica_groups=mesh['dp'=32] {'dp'}, use_global_device_ids=true, to_apply=%add.1 | all-reduce | flops 3072 | bytes 12288
  86.4 40.9 %all-gather.7 = bf16[1,2,384]{1,0,2:T(2,128)(2,1)S(1)} all-gather(bf16[1,2,12]{1,0,2:T(2,128)(2,1)S(1)} %get-tuple-element.278), channel_id=9, replica_groups=mesh['dp'=32] {'dp'}, dimensions={2}, use_global_device_ids=true | all-gather | bytes 1584 | tf_op jit(solution)/shard_map/all_gather | solution.py:202
  129.2 37.4 %all-gather.8 = bf16[1,6,384]{1,0,2:T(2,128)(2,1)S(1)} all-gather(bf16[1,6,12]{1,0,2:T(2,128)(2,1)S(1)} %get-tuple-element.280), channel_id=10, replica_groups=mesh['dp'=32] {'dp'}, dimensions={2}, use_global_device_ids=true | all-gather | bytes 4752 | tf_op jit(solution)/shard_map/all_gather | solution.py:203
  166.8 8.8 slice_reduce_fusion
  175.6 38.7 %all-gather = bf16[1,2,384]{1,0,2:T(2,128)(2,1)S(1)} all-gather(bf16[1,2,12]{1,0,2:T(2,128)(2,1)S(1)} %get-tuple-element.279), channel_id=2, replica_groups=mesh['dp'=32] {'dp'}, dimensions={2}, use_global_device_ids=true | all-gather | bytes 1584 | tf_op jit(solution)/shard_map/all_gather | solution.py:202
  216.2 37.6 %all-gather.1 = bf16[1,6,384]{1,0,2:T(2,128)(2,1)S(1)} all-gather(bf16[1,6,12]{1,0,2:T(2,128)(2,1)S(1)} %get-tuple-element.281), channel_id=3, replica_groups=mesh['dp'=32] {'dp'}, dimensions={2}, use_global_device_ids=true | all-gather | bytes 4752 | tf_op jit(solution)/shard_map/all_gather | solution.py:203
  254.0 8.3 slice_reduce_fusion.8
  262.4 42.4 %all-gather.10 = bf16[1,384,384]{2,0,1:T(2,128)(2,1)} all-gather(bf16[1,12,384]{2,0,1:T(2,128)(2,1)S(1)} %get-tuple-element.275), channel_id=12, replica_groups=mesh['dp'=32] {'dp'}, dimensions={1}, use_global_device_ids=true | all-gather | bytes 304128 | tf_op jit(solution)/shard_map/all_gather | solution.py:206
  304.8 40.9 %all-gather.3 = bf16[1,384,384]{2,0,1:T(2,128)(2,1)} all-gather(bf16[1,12,384]{2,0,1:T(2,128)(2,1)S(1)} %get-tuple-element.276), channel_id=5, replica_groups=mesh['dp'=32] {'dp'}, dimensions={1}, use_global_device_ids=true | all-gather | bytes 304128 | tf_op jit(solution)/shard_map/all_gather | solution.py:206
  346.3 45.5 %all-gather.9 = bf16[1,384,1152]{2,0,1:T(2,128)(2,1)} all-gather(bf16[1,12,1152]{2,0,1:T(2,128)(2,1)S(1)} %get-tuple-element.272), channel_id=11, replica_groups=mesh['dp'=32] {'dp'}, dimensions={1}, use_global_device_ids=true | all-gather | bytes 912384 | tf_op jit(solution)/shard_map/all_gather | solution.py:205
  391.9 42.4 %all-gather.2 = bf16[1,384,1152]{2,0,1:T(2,128)(2,1)S(1)} all-gather(bf16[1,12,1152]{2,0,1:T(2,128)(2,1)S(1)} %get-tuple-element.273), channel_id=4, replica_groups=mesh['dp'=32] {'dp'}, dimensions={1}, use_global_device_ids=true | all-gather | bytes 912384 | tf_op jit(solution)/shard_map/all_gather | solution.py:205
  456.4 6.4 copy.367
  472.6 6.8 reshape.364
  479.4 6.7 copy.369
  486.1 9.0 fusion.132
  495.1 8.7 fusion.16
  504.5 8.2 convert_bitcast_fusion.3
  528.1 11.8 multiply_convert_fusion.3
  540.0 8.6 fusion.134
  562.9 6.8 copy.375
  579.5 6.6 reshape.367
  586.1 6.3 copy.377
  592.4 9.0 fusion.135
  601.4 8.6 fusion.17
  610.1 8.1 convert_bitcast_fusion.2
  621.5 6.3 convert_element_type.218
  634.8 11.7 multiply_convert_fusion.2
  646.5 12.4 fusion.137
  676.4 6.6 reshape.370
  683.0 6.7 copy.383
  689.7 11.3 bitcast_convert_fusion.2
  701.0 10.0 multiply_reduce_fusion.1
  711.0 10.7 multiply_convert_fusion.1
  766.0 6.4 multiply_reduce_fusion.3
  775.0 14.3 %fusion.138 = (f32[1536]{0:T(1024)}, bf16[2364,1536]{1,0:T(8,128)(2,1)S(1)}) fusion(f32[2364,1536]{1,0:T(8,128)} %get-tuple-element.289, bf16[1,1536,384]{2,1,0:T(8,128)(2,1)S(1)} %copy-done.128, f32[2364,384]{1,0:T(8,128)S(1)} %get-tuple-element.257), kind=kOutput, calls=%fused_computation.286 | convolution fusion | flops 2829536256 | bytes 26603520 | tf_op jit(solution)/shard_map/dot_general | solution.py:29
  815.1 10.8 bitcast_convert_fusion
  825.8 10.1 multiply_reduce_fusion
  835.9 10.8 multiply_convert_fusion
  891.3 135.7 %fusion.113 = (f32[16,1152]{1,0:T(8,128)}, f32[16,1152]{1,0:T(8,128)}, f32[16,384]{1,0:T(8,128)}, f32[16,384]{1,0:T(8,128)}, f32[16,1536]{1,0:T(8,128)}, /*index=5*/f32[16,1536]{1,0:T(8,128)}) fusion(f32[384,1152]{1,0:T(8,128)} %fusion.112, f32[384,1152]{1,0:T(8,128)} %fusion.111, f32[384,384]{1,0:T(8,128)S(1)} %copy-done.40, ...), kind=kCustom, calls=%all-reduce-scatter.6 | all-reduce-scatter fusion | flops 3145729 | bytes 9830400
  1033.3 9.9 fusion.110
  1053.2 10.4 multiply_reduce_fusion.5
  1063.6 6.4 collective-permute-start.23
  1073.6 39.8 %all-reduce.21 = (f32[2,384]{1,0:T(2,128)S(1)}, f32[2,384]{1,0:T(2,128)S(1)}, f32[6,384]{1,0:T(8,128)S(1)}, f32[6,384]{1,0:T(8,128)S(1)}, f32[1536]{0:T(1024)S(1)}, /*index=5*/f32[1536]{0:T(1024)S(1)}) all-reduce(f32[2,384]{1,0:T(2,128)S(1)} %pad_maximum_fusion.6, ...), channel_id=17, replica_groups=mesh['dp'=32] {'dp'}, use_global_device_ids=true, to_apply=%region_27.0.clone | all-reduce | flops 9216 | bytes 73728
  1113.7 9.9 fusion.58
  1123.6 8.4 add_multiply_fusion
  1132.2 9.0 fusion.32
  1260.9 7.0 collective-permute-start.38
  (567 shorter events, 411.4 us)
Async XLA Ops:
  7.2 520.9 %all-gather.19.cloned.1.call-start = ((), (), s32[]{:S(2)}) async-start(), calls=%async_computation.4 | async-start | bytes 2433024 | tf_op jit(solution)/shard_map/all_gather | solution.py:207
  9.1 530.8 %all-gather.21.cloned.1.call-start = ((), (), s32[]{:S(2)}) async-start(), calls=%async_computation.5 | async-start | bytes 1216512 | tf_op jit(solution)/shard_map/all_gather | solution.py:208
  10.8 624.0 %all-gather.23.cloned.1.call-start = ((), (), s32[]{:S(2)}) async-start(), calls=%async_computation.6 | async-start | bytes 2433024 | tf_op jit(solution)/shard_map/all_gather | solution.py:207
  11.5 635.0 %all-gather.25.cloned.1.call-start = ((), (), s32[]{:S(2)}) async-start(), calls=%async_computation.7 | async-start | bytes 1216512 | tf_op jit(solution)/shard_map/all_gather | solution.py:208
  12.1 1286.0 %reduce-scatter.21.cloned.1.call-start = ((), (), s32[]{:S(2)}) async-start(), calls=%async_computation.3 | async-start | bytes 2433024 | tf_op jit(solution)/shard_map/reduce_scatter | solution.py:236
  1027.7 119.6 %collective-permute-start.30 = (f32[16,384]{1,0:T(8,128)}, f32[16,384]{1,0:T(8,128)S(1)}, u32[]{:S(2)}, u32[]{:S(2)}) collective-permute-start(f32[16,384]{1,0:T(8,128)} %get-tuple-element.228), channel_id=1, source_target_pairs={{0,7},{1,8},{2,9},{3,10},{4,11},{5,12},{6,13},{7,14},{8,15},{9,16}... | collective-permute-start | bytes 73736
  1029.0 121.8 %collective-permute-start.29 = (f32[16,384]{1,0:T(8,128)}, f32[16,384]{1,0:T(8,128)S(1)}, u32[]{:S(2)}, u32[]{:S(2)}) collective-permute-start(f32[16,384]{1,0:T(8,128)} %get-tuple-element.228), channel_id=1, source_target_pairs={{0,6},{1,7},{2,8},{3,9},{4,10},{5,11},{6,12},{7,13},{8,14},{9,15},... | collective-permute-start | bytes 73736
  1031.6 122.9 %collective-permute-start.28 = (f32[16,384]{1,0:T(8,128)}, f32[16,384]{1,0:T(8,128)S(1)}, u32[]{:S(2)}, u32[]{:S(2)}) collective-permute-start(f32[16,384]{1,0:T(8,128)} %get-tuple-element.228), channel_id=1, source_target_pairs={{0,5},{1,6},{2,7},{3,8},{4,9},{5,10},{6,11},{7,12},{8,13},{9,14},{... | collective-permute-start | bytes 73736
  1043.2 254.9 %reduce-scatter.19.cloned.1.call-start = ((), (), s32[]{:S(2)}) async-start(), calls=%async_computation.2 | async-start | bytes 2433024 | tf_op jit(solution)/shard_map/reduce_scatter | solution.py:236
  1063.6 78.3 %collective-permute-start.23 = (f32[12,384]{1,0:T(8,128)S(1)}, f32[12,384]{1,0:T(8,128)S(1)}, u32[]{:S(2)}, u32[]{:S(2)}) collective-permute-start(f32[12,384]{1,0:T(8,128)S(1)} %slice.226), channel_id=1, source_target_pairs={{0,8},{1,9},{2,10},{3,11},{4,12},{5,13},{6,14},{7,15},{8,16},{9,17... | collective-permute-start | bytes 55304
  1070.1 76.0 %collective-permute-start.31 = (f32[12,384]{1,0:T(8,128)S(1)}, f32[12,384]{1,0:T(8,128)S(1)}, u32[]{:S(2)}, u32[]{:S(2)}) collective-permute-start(f32[12,384]{1,0:T(8,128)S(1)} %slice.227), channel_id=1, source_target_pairs={{0,8},{1,9},{2,10},{3,11},{4,12},{5,13},{6,14},{7,15},{8,16},{9,17... | collective-permute-start | bytes 55304
  1141.9 17.2 %collective-permute-start.27 = (f32[16,384]{1,0:T(8,128)S(1)}, f32[16,384]{1,0:T(8,128)S(1)}, u32[]{:S(2)}, u32[]{:S(2)}) collective-permute-start(f32[16,384]{1,0:T(8,128)S(1)} %copy-done.59), channel_id=1, source_target_pairs={{0,4},{1,5},{2,6},{3,7},{4,8},{5,9},{6,10},{7,11},{8,12},{9,13},{1... | collective-permute-start | bytes 73736
  1146.1 15.5 %collective-permute-start.26 = (f32[16,384]{1,0:T(8,128)S(1)}, f32[16,384]{1,0:T(8,128)S(1)}, u32[]{:S(2)}, u32[]{:S(2)}) collective-permute-start(f32[16,384]{1,0:T(8,128)S(1)} %copy-done.59), channel_id=1, source_target_pairs={{0,3},{1,4},{2,5},{3,6},{4,7},{5,8},{6,9},{7,10},{8,11},{9,12},{10... | collective-permute-start | bytes 73736
  1147.4 16.0 %collective-permute-start.25 = (f32[16,384]{1,0:T(8,128)S(1)}, f32[16,384]{1,0:T(8,128)S(1)}, u32[]{:S(2)}, u32[]{:S(2)}) collective-permute-start(f32[16,384]{1,0:T(8,128)S(1)} %copy-done.59), channel_id=1, source_target_pairs={{0,2},{1,3},{2,4},{3,5},{4,6},{5,7},{6,8},{7,9},{8,10},{9,11},{10,... | collective-permute-start | bytes 73736
  1150.8 16.2 %collective-permute-start.24 = (f32[16,384]{1,0:T(8,128)S(1)}, f32[16,384]{1,0:T(8,128)S(1)}, u32[]{:S(2)}, u32[]{:S(2)}) collective-permute-start(f32[16,384]{1,0:T(8,128)S(1)} %copy-done.59), channel_id=1, source_target_pairs={{0,1},{1,2},{2,3},{3,4},{4,5},{5,6},{6,7},{7,8},{8,9},{9,10},{10,1... | collective-permute-start | bytes 73736
  1154.6 14.1 %collective-permute-start.22 = (f32[16,384]{1,0:T(8,128)S(1)}, f32[16,384]{1,0:T(8,128)S(1)}, u32[]{:S(2)}, u32[]{:S(2)}) collective-permute-start(f32[16,384]{1,0:T(8,128)S(1)} %copy-done.58), channel_id=1, source_target_pairs={{0,7},{1,8},{2,9},{3,10},{4,11},{5,12},{6,13},{7,14},{8,15},{9,16}... | collective-permute-start | bytes 73736
  1159.1 14.0 %collective-permute-start.21 = (f32[16,384]{1,0:T(8,128)S(1)}, f32[16,384]{1,0:T(8,128)S(1)}, u32[]{:S(2)}, u32[]{:S(2)}) collective-permute-start(f32[16,384]{1,0:T(8,128)S(1)} %copy-done.58), channel_id=1, source_target_pairs={{0,6},{1,7},{2,8},{3,9},{4,10},{5,11},{6,12},{7,13},{8,14},{9,15},... | collective-permute-start | bytes 73736
  1161.6 12.9 collective-permute-start.20
  1163.3 12.5 collective-permute-start.19
  1167.0 34.3 %collective-permute-start.18 = (f32[16,384]{1,0:T(8,128)S(1)}, f32[16,384]{1,0:T(8,128)S(1)}, u32[]{:S(2)}, u32[]{:S(2)}) collective-permute-start(f32[16,384]{1,0:T(8,128)S(1)} %copy-done.58), channel_id=1, source_target_pairs={{0,3},{1,4},{2,5},{3,6},{4,7},{5,8},{6,9},{7,10},{8,11},{9,12},{10... | collective-permute-start | bytes 73736
  1168.7 35.3 %collective-permute-start.17 = (f32[16,384]{1,0:T(8,128)S(1)}, f32[16,384]{1,0:T(8,128)S(1)}, u32[]{:S(2)}, u32[]{:S(2)}) collective-permute-start(f32[16,384]{1,0:T(8,128)S(1)} %copy-done.58), channel_id=1, source_target_pairs={{0,2},{1,3},{2,4},{3,5},{4,6},{5,7},{6,8},{7,9},{8,10},{9,11},{10,... | collective-permute-start | bytes 73736
  1173.2 33.5 %collective-permute-start.16 = (f32[16,384]{1,0:T(8,128)S(1)}, f32[16,384]{1,0:T(8,128)S(1)}, u32[]{:S(2)}, u32[]{:S(2)}) collective-permute-start(f32[16,384]{1,0:T(8,128)S(1)} %copy-done.58), channel_id=1, source_target_pairs={{0,1},{1,2},{2,3},{3,4},{4,5},{5,6},{6,7},{7,8},{8,9},{9,10},{10,1... | collective-permute-start | bytes 73736
  1174.5 35.7 %collective-permute-start.7 = (f32[12,1152]{1,0:T(8,128)S(1)}, f32[12,1152]{1,0:T(8,128)S(1)}, u32[]{:S(2)}, u32[]{:S(2)}) collective-permute-start(f32[12,1152]{1,0:T(8,128)S(1)} %slice.224), channel_id=1, source_target_pairs={{0,8},{1,9},{2,10},{3,11},{4,12},{5,13},{6,14},{7,15},{8,16},{9,17... | collective-permute-start | bytes 165896
  1175.9 35.9 %collective-permute-start.15 = (f32[12,1152]{1,0:T(8,128)S(1)}, f32[12,1152]{1,0:T(8,128)S(1)}, u32[]{:S(2)}, u32[]{:S(2)}) collective-permute-start(f32[12,1152]{1,0:T(8,128)S(1)} %slice.225), channel_id=1, source_target_pairs={{0,8},{1,9},{2,10},{3,11},{4,12},{5,13},{6,14},{7,15},{8,16},{9,17... | collective-permute-start | bytes 165896
  1201.3 12.2 collective-permute-start.14
  1204.1 13.4 %collective-permute-start.13 = (f32[16,1152]{1,0:T(8,128)S(1)}, f32[16,1152]{1,0:T(8,128)S(1)}, u32[]{:S(2)}, u32[]{:S(2)}) collective-permute-start(f32[16,1152]{1,0:T(8,128)S(1)} %copy-done.50), channel_id=1, source_target_pairs={{0,6},{1,7},{2,8},{3,9},{4,10},{5,11},{6,12},{7,13},{8,14},{9,15},... | collective-permute-start | bytes 221192
  1206.6 12.1 collective-permute-start.12
  1210.2 11.7 collective-permute-start.11
  1211.8 11.5 collective-permute-start.10
  1213.5 12.3 collective-permute-start.9
  1225.8 13.7 %collective-permute-start.3 = (f32[16,1152]{1,0:T(8,128)S(1)}, f32[16,1152]{1,0:T(8,128)S(1)}, u32[]{:S(2)}, u32[]{:S(2)}) collective-permute-start(f32[16,1152]{1,0:T(8,128)S(1)} %copy-done.49), channel_id=1, source_target_pairs={{0,4},{1,5},{2,6},{3,7},{4,8},{5,9},{6,10},{7,11},{8,12},{9,13},{1... | collective-permute-start | bytes 221192
  1227.2 14.9 %collective-permute-start.2 = (f32[16,1152]{1,0:T(8,128)S(1)}, f32[16,1152]{1,0:T(8,128)S(1)}, u32[]{:S(2)}, u32[]{:S(2)}) collective-permute-start(f32[16,1152]{1,0:T(8,128)S(1)} %copy-done.49), channel_id=1, source_target_pairs={{0,3},{1,4},{2,5},{3,6},{4,7},{5,8},{6,9},{7,10},{8,11},{9,12},{10... | collective-permute-start | bytes 221192
  1230.0 13.7 %collective-permute-start.1 = (f32[16,1152]{1,0:T(8,128)S(1)}, f32[16,1152]{1,0:T(8,128)S(1)}, u32[]{:S(2)}, u32[]{:S(2)}) collective-permute-start(f32[16,1152]{1,0:T(8,128)S(1)} %copy-done.49), channel_id=1, source_target_pairs={{0,2},{1,3},{2,4},{3,5},{4,6},{5,7},{6,8},{7,9},{8,10},{9,11},{10,... | collective-permute-start | bytes 221192
  1233.1 12.2 collective-permute-start
  1234.4 13.5 %collective-permute-start.39 = (f32[12,1536]{1,0:T(8,128)S(1)}, f32[12,1536]{1,0:T(8,128)S(1)}, u32[]{:S(2)}, u32[]{:S(2)}) collective-permute-start(f32[12,1536]{1,0:T(8,128)S(1)} %slice.228), channel_id=1, source_target_pairs={{0,8},{1,9},{2,10},{3,11},{4,12},{5,13},{6,14},{7,15},{8,16},{9,17... | collective-permute-start | bytes 221192
  1239.5 14.6 %collective-permute-start.46 = (f32[16,1536]{1,0:T(8,128)S(1)}, f32[16,1536]{1,0:T(8,128)S(1)}, u32[]{:S(2)}, u32[]{:S(2)}) collective-permute-start(f32[16,1536]{1,0:T(8,128)S(1)} %copy-done.48), channel_id=1, source_target_pairs={{0,7},{1,8},{2,9},{3,10},{4,11},{5,12},{6,13},{7,14},{8,15},{9,16}... | collective-permute-start | bytes 294920
  1242.1 17.4 %collective-permute-start.45 = (f32[16,1536]{1,0:T(8,128)S(1)}, f32[16,1536]{1,0:T(8,128)S(1)}, u32[]{:S(2)}, u32[]{:S(2)}) collective-permute-start(f32[16,1536]{1,0:T(8,128)S(1)} %copy-done.48), channel_id=1, source_target_pairs={{0,6},{1,7},{2,8},{3,9},{4,10},{5,11},{6,12},{7,13},{8,14},{9,15},... | collective-permute-start | bytes 294920
  1243.7 17.2 %collective-permute-start.44 = (f32[16,1536]{1,0:T(8,128)S(1)}, f32[16,1536]{1,0:T(8,128)S(1)}, u32[]{:S(2)}, u32[]{:S(2)}) collective-permute-start(f32[16,1536]{1,0:T(8,128)S(1)} %copy-done.48), channel_id=1, source_target_pairs={{0,5},{1,6},{2,7},{3,8},{4,9},{5,10},{6,11},{7,12},{8,13},{9,14},{... | collective-permute-start | bytes 294920
  1245.3 22.6 %collective-permute-start.43 = (f32[16,1536]{1,0:T(8,128)S(1)}, f32[16,1536]{1,0:T(8,128)S(1)}, u32[]{:S(2)}, u32[]{:S(2)}) collective-permute-start(f32[16,1536]{1,0:T(8,128)S(1)} %copy-done.48), channel_id=1, source_target_pairs={{0,4},{1,5},{2,6},{3,7},{4,8},{5,9},{6,10},{7,11},{8,12},{9,13},{1... | collective-permute-start | bytes 294920
  1251.7 17.5 %collective-permute-start.42 = (f32[16,1536]{1,0:T(8,128)S(1)}, f32[16,1536]{1,0:T(8,128)S(1)}, u32[]{:S(2)}, u32[]{:S(2)}) collective-permute-start(f32[16,1536]{1,0:T(8,128)S(1)} %copy-done.48), channel_id=1, source_target_pairs={{0,3},{1,4},{2,5},{3,6},{4,7},{5,8},{6,9},{7,10},{8,11},{9,12},{10... | collective-permute-start | bytes 294920
  1254.1 17.0 %collective-permute-start.41 = (f32[16,1536]{1,0:T(8,128)S(1)}, f32[16,1536]{1,0:T(8,128)S(1)}, u32[]{:S(2)}, u32[]{:S(2)}) collective-permute-start(f32[16,1536]{1,0:T(8,128)S(1)} %copy-done.48), channel_id=1, source_target_pairs={{0,2},{1,3},{2,4},{3,5},{4,6},{5,7},{6,8},{7,9},{8,10},{9,11},{10,... | collective-permute-start | bytes 294920
  1259.5 14.1 %collective-permute-start.40 = (f32[16,1536]{1,0:T(8,128)S(1)}, f32[16,1536]{1,0:T(8,128)S(1)}, u32[]{:S(2)}, u32[]{:S(2)}) collective-permute-start(f32[16,1536]{1,0:T(8,128)S(1)} %copy-done.48), channel_id=1, source_target_pairs={{0,1},{1,2},{2,3},{3,4},{4,5},{5,6},{6,7},{7,8},{8,9},{9,10},{10,1... | collective-permute-start | bytes 294920
  1260.9 15.7 %collective-permute-start.38 = (f32[16,1536]{1,0:T(8,128)S(1)}, f32[16,1536]{1,0:T(8,128)S(1)}, u32[]{:S(2)}, u32[]{:S(2)}) collective-permute-start(f32[16,1536]{1,0:T(8,128)S(1)} %copy-done.47), channel_id=1, source_target_pairs={{0,7},{1,8},{2,9},{3,10},{4,11},{5,12},{6,13},{7,14},{8,15},{9,16}... | collective-permute-start | bytes 294920
  1267.9 12.0 collective-permute-start.37
  1269.2 18.5 %collective-permute-start.36 = (f32[16,1536]{1,0:T(8,128)S(1)}, f32[16,1536]{1,0:T(8,128)S(1)}, u32[]{:S(2)}, u32[]{:S(2)}) collective-permute-start(f32[16,1536]{1,0:T(8,128)S(1)} %copy-done.47), channel_id=1, source_target_pairs={{0,5},{1,6},{2,7},{3,8},{4,9},{5,10},{6,11},{7,12},{8,13},{9,14},{... | collective-permute-start | bytes 294920
  1271.2 16.6 %collective-permute-start.35 = (f32[16,1536]{1,0:T(8,128)S(1)}, f32[16,1536]{1,0:T(8,128)S(1)}, u32[]{:S(2)}, u32[]{:S(2)}) collective-permute-start(f32[16,1536]{1,0:T(8,128)S(1)} %copy-done.47), channel_id=1, source_target_pairs={{0,4},{1,5},{2,6},{3,7},{4,8},{5,9},{6,10},{7,11},{8,12},{9,13},{1... | collective-permute-start | bytes 294920
  1273.7 14.2 %collective-permute-start.34 = (f32[16,1536]{1,0:T(8,128)S(1)}, f32[16,1536]{1,0:T(8,128)}, u32[]{:S(2)}, u32[]{:S(2)}) collective-permute-start(f32[16,1536]{1,0:T(8,128)S(1)} %copy-done.47), channel_id=1, source_target_pairs={{0,3},{1,4},{2,5},{3,6},{4,7},{5,8},{6,9},{7,10},{8,11},{9,12},{10... | collective-permute-start | bytes 294920
  1276.6 11.2 collective-permute-start.33
  (138 other events, 3691.4 us)
Sparse Core Ops, SparseCore 0:
  11.5 59.8 all-gather.18
  74.9 52.6 all-gather.20
  131.0 56.3 all-gather.22
  190.8 52.8 all-gather.24
  1043.3 103.1 reduce-scatter.20
  1151.6 106.3 reduce-scatter.18
where the time goes:
time: 1320 us; the launch traced here: 1310 us
  blocking collectives  544 us (41%)
  local copies, waits for them, and re-layouts  267 us (20%)
  matrix products  252 us (19%)
  starting transfers between devices  124 us (9%)
  other arithmetic  100 us (8%)
  between operations  16.9 us (1%)
    unnamed x3, blocking collectives  218 us
    unnamed x48, starting transfers between devices  124 us
    dot_general x12, matrix products, mixed(): return jnp.einsum(form, left, right, preferred_element_type=jnp.float32)  92.3 us
    all_gather x2, blocking collectives, fetch_layer(): lax.all_gather(qkv_part, 'dp', axis=0, tiled=True)  88 us
    all_gather x2, blocking collectives, fetch_layer(): lax.all_gather(outw_part, 'dp', axis=0, tiled=True)  83.3 us
    all_gather x2, blocking collectives, fetch_layer(): lax.all_gather(gain_part, 'dp', axis=1, tiled=True)  79.5 us
    all_gather x2, blocking collectives, fetch_layer(): lax.all_gather(shift_part, 'dp', axis=1, tiled=True)  75 us
    dot_general x8, matrix products, back_dot(): lax.dot_general(left, weight, (((1,), (1,)), ((), ())), preferred_element...  57.8 us
  transfers between devices with their start and end apart: 54, of which 1 were waited for; matrix products, arithmetic and copies ran while one was open for 28% of the time, Pallas kernels for 0%

commit v1 on v0

v1 whole, which is shorter than its diff:
```python
import functools

import jax
import jax.numpy as jnp
import numpy as np
from jax import lax
from jax.experimental import pallas as pl
from jax.experimental.pallas import tpu as pltpu
from jax.sharding import PartitionSpec as P

HD = 64
STEP = 3
LANES = 128

BETA_ONE = 0.9
BETA_TWO = 0.95
LEARN_RATE = 0.02
DECAY = 0.05
ADAM_EPS = 1e-08
NORM_EPS = 1e-06

BF = jnp.bfloat16
F4 = jnp.float32
VMEM_LIMIT = 63 * 1024 * 1024


def dot_nn(a, b):
    return lax.dot_general(a, b, (((1,), (0,)), ((), ())), preferred_element_type=F4)


def dot_nt(a, b):
    return lax.dot_general(a, b, (((1,), (1,)), ((), ())), preferred_element_type=F4)


def dot_tn(a, b):
    return lax.dot_general(a, b, (((0,), (0,)), ((), ())), preferred_element_type=F4)


def col_sum(x):
    return jnp.sum(x, axis=0, keepdims=True)


def normalize(rows, gain, shift):
    center = rows - jnp.mean(rows, axis=-1, keepdims=True)
    rstd = lax.rsqrt(jnp.mean(center * center, axis=-1, keepdims=True) + NORM_EPS)
    normed = center * rstd
    return (normed * gain + shift, normed, rstd)


def norm_back(grad_in, gain, normed, rstd):
    scaled = grad_in * gain
    return rstd * (
        scaled
        - jnp.mean(scaled, axis=-1, keepdims=True)
        - normed * jnp.mean(scaled * normed, axis=-1, keepdims=True)
    )


class Sizes:
    def __init__(self, n, images, seq, width, hidden, layers):
        assert n & (n - 1) == 0 and width % n == 0 and hidden % n == 0
        self.n, self.images, self.seq = n, images, seq
        self.width, self.hidden, self.layers = width, hidden, layers
        self.heads = width // HD
        self.rows = -(-seq // 16) * 16
        self.bits = n.bit_length() - 1
        self.kr, self.kd, self.ku = width // n, hidden // n, hidden // n
        cb = width // LANES
        self.segs = []
        at = 0
        for name, blocks, rows in (
            ("q", 3 * cb, self.kr),
            ("o", cb, self.kr),
            ("u", hidden // LANES, self.kr),
            ("d", cb, self.kd),
        ):
            self.segs.append((name, blocks, rows, at))
            at += blocks * rows
        self.small = -(-at // 8) * 8
        self.pack = self.small + 8
        third = -(-self.pack // 24) * 8
        self.parts = [(0, third), (third, third), (2 * third, self.pack - 2 * third)]
        mid = [1 << b for b in range(self.bits - 2, 0, -1)]
        top = [1 << (self.bits - 1)]
        self.orders = []
        for i in range(3):
            turn = (i * len(mid)) // 3
            self.orders.append(top + mid[turn:] + mid[:turn] + [1])
        self.group = 1
        while self.group * self.kr % 16:
            self.group *= 2

    def place(self, part):
        order = self.orders[part]
        out = []
        for rel in range(self.n):
            out.append(sum(((rel // b) & 1) << s for s, b in enumerate(order)))
        return out


def spec_any():
    return pl.BlockSpec(memory_space=pl.ANY)


def lane_iota():
    return lax.broadcasted_iota(jnp.int32, (8, LANES), 1)


def pack_kernel(sz, gain, bias, upb, wq, wo, wu, wd, *refs):
    outs, st = refs[:-1], refs[-1]
    src = {"q": wq, "o": wo, "u": wu, "d": wd}
    st[...] = jnp.zeros_like(st)
    for layer in range(sz.layers):
        for name, blocks, rows, at in sz.segs:
            for c in range(blocks):
                st[at + c * rows : at + (c + 1) * rows, :] = src[name][
                    layer, :, c * LANES : (c + 1) * LANES
                ]
        s = sz.small
        st[s : s + 2, 0 : sz.kr] = gain[layer]
        st[s + 2 : s + 8, 0 : sz.kr] = bias[layer]
        st[s : s + 1, 64 : 64 + sz.ku] = upb[layer : layer + 1, :]
        for p, (first, count) in enumerate(sz.parts):
            outs[layer * 3 + p][...] = st[first : first + count, :].astype(BF)


def pack_params(sz, params):
    shapes = [
        jax.ShapeDtypeStruct((count, LANES), BF)
        for _ in range(sz.layers)
        for _, count in sz.parts
    ]
    flat = pl.pallas_call(
        functools.partial(pack_kernel, sz),
        out_shape=shapes,
        scratch_shapes=[pltpu.VMEM((sz.pack, LANES), F4)],
        name="pack",
    )(*params)
    return [flat[3 * i : 3 * i + 3] for i in range(sz.layers)]


def swap(x, bit, n):
    return lax.ppermute(x, "dp", [(i, i ^ bit) for i in range(n)])


def gather_parts(sz, parts):
    held = [p[None] for p in parts]
    for s in range(sz.bits - 1):
        got = [swap(h, sz.orders[i][s], sz.n) for i, h in enumerate(held)]
        held = [jnp.concatenate([h, g], axis=0) for h, g in zip(held, got)]
    got = [swap(h, sz.orders[i][-1], sz.n) for i, h in enumerate(held)]
    return [x for pair in zip(held, got) for x in pair]


def scatter_parts(sz, halves):
    pairs = [tuple(halves[2 * i : 2 * i + 2]) for i in range(3)]
    for s in range(sz.bits - 1, 0, -1):
        got = [swap(send, sz.orders[i][s], sz.n) for i, (_, send) in enumerate(pairs)]
        half = (1 << s) // 2
        pairs = [
            (keep[:half] + g[:half], keep[half:] + g[half:])
            for (keep, _), g in zip(pairs, got)
        ]
    got = [swap(send, sz.orders[i][0], sz.n) for i, (_, send) in enumerate(pairs)]
    return [x for (keep, _), g in zip(pairs, got) for x in (keep, g)]


def read_weights(sz, tab, halves, gbuf, w, st, st_w, sems):
    half = sz.n // 2
    copies = []
    for p, (first, count) in enumerate(sz.parts):
        for side in range(2):
            copy = pltpu.make_async_copy(
                halves[2 * p + side],
                gbuf.at[pl.ds(side * half, half), pl.ds(first, count), :],
                sems.at[2 * p + side],
            )
            copy.start()
            copies.append(copy)
    for copy in copies:
        copy.wait()
    lane = lane_iota()
    span = sz.group

    @pl.loop(0, sz.n // span)
    def _(grp):
        for j in range(span):
            d = grp * span + j
            for p, (first, count) in enumerate(sz.parts):
                st[first : first + count, :] = gbuf[
                    tab[p * sz.n + d], first : first + count, :
                ].astype(F4)
            slot = 0
            for name, blocks, rows, at in sz.segs:
                for c in range(blocks):
                    st_w[slot, j * rows : (j + 1) * rows, :] = st[
                        at + c * rows : at + (c + 1) * rows, :
                    ]
                    slot += 1
        slot = 0
        for name, blocks, rows, at in sz.segs:
            base = pl.multiple_of(grp * (span * rows), 16)
            for c in range(blocks):
                w[name][pl.ds(base, span * rows), c * LANES : (c + 1) * LANES] = st_w[
                    slot, 0 : span * rows, :
                ].astype(BF)
                slot += 1

    last = 2
    gains = [jnp.zeros((8, LANES), F4) for _ in range(sz.width // LANES)]
    ups = [jnp.zeros((8, LANES), F4) for _ in range(sz.hidden // LANES)]
    for d in range(sz.n):
        v = gbuf[tab[last * sz.n + d], sz.small : sz.small + 8, :].astype(F4)
        for tiles, width, src in ((gains, sz.kr, 0), (ups, sz.ku, 64)):
            dst = d * width
            moved = pltpu.roll(v, (dst - src) % LANES, 1)
            for t in range(dst // LANES, (dst + width - 1) // LANES + 1):
                lo, hi = dst - t * LANES, dst + width - t * LANES
                tiles[t] = jnp.where((lane >= lo) & (lane < hi), moved, tiles[t])
    for t, tile in enumerate(gains):
        w["g"][:, t * LANES : (t + 1) * LANES] = tile
    for t, tile in enumerate(ups):
        w["b"][:, t * LANES : (t + 1) * LANES] = tile


def write_grads(sz, tab, acc, obuf, outs, st, sems):
    span = sz.group

    @pl.loop(0, sz.n // span)
    def _(grp):
        for j in range(span):
            d = grp * span + j
            for name, blocks, rows, at in sz.segs:
                base = pl.multiple_of(grp * (span * rows), 16)
                for c in range(blocks):
                    st[at + c * rows : at + (c + 1) * rows, :] = acc[name][
                        pl.ds(base, span * rows), c * LANES : (c + 1) * LANES
                    ][j * rows : (j + 1) * rows, :]
            for p, (first, count) in enumerate(sz.parts):
                stop = min(first + count, sz.small)
                obuf[tab[p * sz.n + d], first:stop, :] = st[first:stop, :].astype(BF)

    lane = lane_iota()
    row = lax.broadcasted_iota(jnp.int32, (8, LANES), 0)
    for d in range(sz.n):
        out = jnp.zeros((8, LANES), F4)
        for name, width, src in (("g", sz.kr, 0), ("b", sz.ku, 64)):
            dst = d * width
            for t in range(dst // LANES, (dst + width - 1) // LANES + 1):
                lo = max(dst - t * LANES, 0) - (dst - t * LANES) + src
                hi = min(dst + width - t * LANES, LANES) - (dst - t * LANES) + src
                tile = acc[name][:, t * LANES : (t + 1) * LANES]
                moved = pltpu.roll(tile, (src - dst) % LANES, 1)
                here = (lane >= lo) & (lane < hi)
                if name == "b":
                    here = here & (row == 0)
                out = jnp.where(here, moved, out)
        obuf[tab[2 * sz.n + d], sz.small : sz.small + 8, :] = out.astype(BF)

    half = sz.n // 2
    copies = []
    for p, (first, count) in enumerate(sz.parts):
        for side in range(2):
            copy = pltpu.make_async_copy(
                obuf.at[pl.ds(side * half, half), pl.ds(first, count), :],
                outs[2 * p + side],
                sems.at[2 * p + side],
            )
            copy.start()
            copies.append(copy)
    for copy in copies:
        copy.wait()


def half_mask(h):
    lane = lax.broadcasted_iota(jnp.int32, (1, LANES), 1)
    low = lane < HD
    return low if h % 2 == 0 else jnp.logical_not(low)


def head_of(ref, h):
    pair = ref[:, (h // 2) * LANES : (h // 2 + 1) * LANES]
    return jnp.where(half_mask(h), pair, jnp.zeros_like(pair))


def pair_of(ref, h):
    return ref[:, (h // 2) * LANES : (h // 2 + 1) * LANES]


def forward_image(sz, x, w, s):
    D = sz.width
    scale = HD ** (-0.5)
    g = w["g"]
    a1f, xn1, r1 = normalize(x, g[0:1, :], g[2:3, :])
    a1 = a1f.astype(BF)
    s["xn1"][...] = xn1
    s["r1"][...] = r1
    s["a1"][...] = a1
    s["q"][...] = ((dot_nn(a1, w["q"][:, 0:D]) + g[3:4, :]) * scale).astype(BF)
    s["k"][...] = dot_nn(a1, w["q"][:, D : 2 * D]).astype(BF)
    v = dot_nn(a1, w["q"][:, 2 * D : 3 * D]) + g[4:5, :]
    s["v"][...] = v.astype(BF)
    s["vt"][...] = v.T.astype(BF)
    row = lax.broadcasted_iota(jnp.int32, (sz.rows, 1), 0)
    for h in range(sz.heads):
        sc = dot_nt(pair_of(s["k"], h), head_of(s["q"], h))
        sc = jnp.where(row < sz.seq, sc, -1e30)
        top = jnp.max(sc, axis=0, keepdims=True)
        expo = jnp.exp(sc - top)
        total = jnp.sum(expo, axis=0, keepdims=True)
        probs = expo * (1.0 / total)
        s["p"][h] = probs
        s["ct"][h * HD : (h + 1) * HD, :] = dot_nn(
            s["vt"][h * HD : (h + 1) * HD, :], probs.astype(BF)
        )
    ctx = s["ct"][...].T.astype(BF)
    s["ctx"][...] = ctx
    h_res = x + dot_nn(ctx, w["o"][...]) + g[5:6, :]
    a2f, xn2, r2 = normalize(h_res, g[1:2, :], g[6:7, :])
    a2 = a2f.astype(BF)
    s["xn2"][...] = xn2
    s["r2"][...] = r2
    s["a2"][...] = a2
    u = dot_nn(a2, w["u"][...]) + w["b"][0:1, :]
    one_erf = 0.5 * (1.0 + lax.erf(u * 0.7071067811865476))
    s["z"][...] = (u * one_erf).astype(BF)
    s["gp"][...] = one_erf + u * jnp.exp(-0.5 * u * u) * 0.3989422804014327
    return h_res + dot_nn(s["z"][...], w["d"][...]) + g[7:8, :]


def backward_image(sz, dy, w, s, acc, t):
    D = sz.width
    scale = HD ** (-0.5)
    g = w["g"]
    dyb = dy.astype(BF)
    acc["d"][...] += dot_tn(s["z"][...], dyb)
    acc["g"][7:8, :] += col_sum(dy)
    du = dot_nt(dyb, w["d"][...]) * s["gp"][...]
    acc["b"][0:1, :] += col_sum(du)
    t["dub"][...] = du.astype(BF)
    dub = t["dub"][...]
    acc["u"][...] += dot_tn(s["a2"][...], dub)
    da2 = dot_nt(dub, w["u"][...])
    xn2 = s["xn2"][...]
    acc["g"][1:2, :] += col_sum(da2 * xn2)
    acc["g"][6:7, :] += col_sum(da2)
    dh = dy + norm_back(da2, g[1:2, :], xn2, s["r2"][...])
    dhb = dh.astype(BF)
    acc["o"][...] += dot_tn(s["ctx"][...], dhb)
    acc["g"][5:6, :] += col_sum(dh)
    t["dc"][...] = dot_nt(dhb, w["o"][...]).astype(BF)
    t["kt"][...] = s["k"][...].astype(F4).T.astype(BF)
    for pair in range(sz.heads // 2):
        dv = dk = None
        for h in (2 * pair, 2 * pair + 1):
            dch, qh = head_of(t["dc"], h), head_of(s["q"], h)
            dp = dot_nt(pair_of(s["v"], h), dch)
            probs = s["p"][h]
            inner = jnp.sum(probs * dp, axis=0, keepdims=True)
            ds = (probs * (dp - inner)).astype(BF)
            dvh, dkh = dot_nn(probs.astype(BF), dch), dot_nn(ds, qh)
            dv = dvh if dv is None else dv + dvh
            dk = dkh if dk is None else dk + dkh
            t["qt"][h * HD : (h + 1) * HD, :] = dot_nn(t["kt"][h * HD : (h + 1) * HD, :], ds) * scale
        at = pair * LANES
        acc["g"][4:5, at : at + LANES] += col_sum(dv)
        t["dp"][:, D + at : D + at + LANES] = dk.astype(BF)
        t["dp"][:, 2 * D + at : 2 * D + at + LANES] = dv.astype(BF)
    dq = t["qt"][...].T
    acc["g"][3:4, :] += col_sum(dq)
    t["dp"][:, 0:D] = dq.astype(BF)
    dproj = t["dp"][...]
    acc["q"][...] += dot_tn(s["a1"][...], dproj)
    dfirst = dot_nt(dproj, w["q"][...])
    xn1 = s["xn1"][...]
    acc["g"][0:1, :] += col_sum(dfirst * xn1)
    acc["g"][2:3, :] += col_sum(dfirst)
    return dh + norm_back(dfirst, g[0:1, :], xn1, s["r1"][...])


WEIGHTS = ("q", "o", "u", "d", "g", "b")
SAVED = ("xn1", "r1", "a1", "q", "k", "v", "p", "ctx", "xn2", "r2", "a2", "z", "gp")
TEMPS = ("dub", "dc", "kt", "qt", "dp")


def weight_scratch(sz, kind):
    D, FF = sz.width, sz.hidden
    return [
        pltpu.VMEM((D, 3 * D), kind),
        pltpu.VMEM((D, D), kind),
        pltpu.VMEM((D, FF), kind),
        pltpu.VMEM((FF, D), kind),
        pltpu.VMEM((8, D), F4),
        pltpu.VMEM((8, FF), F4),
    ]


def load_scratch(sz):
    most = max(rows for _, _, rows, _ in sz.segs) * sz.group
    slots = sum(blocks for _, blocks, _, _ in sz.segs)
    return [
        pltpu.VMEM((sz.n, sz.pack, LANES), BF),
        pltpu.VMEM((sz.pack, LANES), F4),
        pltpu.VMEM((slots, most, LANES), F4),
        pltpu.SemaphoreType.DMA((6,)),
    ]


def saved_shapes(sz):
    R, D, FF = sz.rows, sz.width, sz.hidden
    return {
        "xn1": ((R, D), F4),
        "r1": ((R, 1), F4),
        "a1": ((R, D), BF),
        "q": ((R, D), BF),
        "k": ((R, D), BF),
        "v": ((R, D), BF),
        "p": ((sz.heads, R, R), F4),
        "ctx": ((R, D), BF),
        "xn2": ((R, D), F4),
        "r2": ((R, 1), F4),
        "a2": ((R, D), BF),
        "z": ((R, FF), BF),
        "gp": ((R, FF), F4),
    }


def local_shapes(sz):
    R, D, FF = sz.rows, sz.width, sz.hidden
    return {"vt": ((D, R), BF), "ct": ((D, R), F4)}


def temp_shapes(sz):
    R, D, FF = sz.rows, sz.width, sz.hidden
    return {
        "dub": ((R, FF), BF),
        "dc": ((R, D), BF),
        "kt": ((D, R), BF),
        "qt": ((D, R), F4),
        "dp": ((R, 3 * D), BF),
    }


def named(names, refs):
    return dict(zip(names, refs))


def first_kernel(sz, tab, tokens, *refs):
    refs = list(refs)
    take = lambda k: [refs.pop(0) for _ in range(k)]
    halves = take(6)
    (x1,) = take(1)
    saved = {k: r.at[0] for k, r in named(SAVED, take(len(SAVED))).items()}
    w = named(WEIGHTS, take(6))
    gbuf, st, st_w, sems = take(4)
    (xs,) = take(1)
    local = named(("vt", "ct"), take(2))
    i = pl.program_id(0)

    @pl.when(i == 0)
    def _():
        read_weights(sz, tab, halves, gbuf, w, st, st_w, sems)
        xs[...] = jnp.zeros_like(xs)

    @pl.when(tab[3 * sz.n + i] == 1)
    def _():
        xs[0 : sz.seq, :] = tokens[0].astype(F4)
        x1[0] = forward_image(sz, xs[...], w, {**saved, **local})


def second_kernel(sz, tab, x1, cot, *refs):
    refs = list(refs)
    take = lambda k: [refs.pop(0) for _ in range(k)]
    halves = take(6)
    out, dx = take(2)
    packed = take(6)
    w = named(WEIGHTS, take(6))
    acc = named(WEIGHTS, take(6))
    gbuf, st, st_w, sems = take(4)
    (dys,) = take(1)
    saved = named(SAVED, take(len(SAVED)))
    local = named(("vt", "ct"), take(2))
    temps = named(TEMPS, take(5))
    i = pl.program_id(0)

    @pl.when(i == 0)
    def _():
        read_weights(sz, tab, halves, gbuf, w, st, st_w, sems)
        for name in WEIGHTS:
            acc[name][...] = jnp.zeros_like(acc[name])
        dys[...] = jnp.zeros_like(dys)

    live = tab[3 * sz.n + i] == 1

    @pl.when(live)
    def _():
        s = {**saved, **local}
        y = forward_image(sz, x1[0], w, s)
        out[0] = y[0 : sz.seq, :]
        dys[0 : sz.seq, :] = cot[0]
        dx[0] = backward_image(sz, dys[...], w, s, acc, temps)

    @pl.when(jnp.logical_not(live))
    def _():
        out[0] = jnp.zeros(out.shape[1:], F4)

    @pl.when(i == sz.images - 1)
    def _():
        write_grads(sz, tab, acc, gbuf, packed, st, sems)


def third_kernel(sz, tab, dx, *refs):
    refs = list(refs)
    take = lambda k: [refs.pop(0) for _ in range(k)]
    saved = {k: r.at[0] for k, r in named(SAVED, take(len(SAVED))).items()}
    halves = take(6)
    (out,) = take(1)
    packed = take(6)
    w = named(WEIGHTS, take(6))
    acc = named(WEIGHTS, take(6))
    gbuf, st, st_w, sems = take(4)
    temps = named(TEMPS, take(5))
    i = pl.program_id(0)

    @pl.when(i == 0)
    def _():
        read_weights(sz, tab, halves, gbuf, w, st, st_w, sems)
        for name in WEIGHTS:
            acc[name][...] = jnp.zeros_like(acc[name])

    live = tab[3 * sz.n + i] == 1

    @pl.when(live)
    def _():
        out[0] = backward_image(sz, dx[0], w, saved, acc, temps)[0 : sz.seq, :]

    @pl.when(jnp.logical_not(live))
    def _():
        out[0] = jnp.zeros(out.shape[1:], F4)

    @pl.when(i == sz.images - 1)
    def _():
        write_grads(sz, tab, acc, gbuf, packed, st, sems)


def image_spec(shape):
    zeros = (0,) * len(shape)
    return pl.BlockSpec((1,) + tuple(shape), lambda i, tab: (i,) + zeros)


def scratch_of(shapes, names):
    return [pltpu.VMEM(*shapes[k]) for k in names]


def packed_outs(sz):
    return [
        jax.ShapeDtypeStruct((sz.n // 2, count, LANES), BF)
        for _, count in sz.parts
        for _ in range(2)
    ]


def params():
    return pltpu.CompilerParams(
        dimension_semantics=("arbitrary",), vmem_limit_bytes=VMEM_LIMIT
    )


def run_first(sz, tab, tokens, halves):
    saved = saved_shapes(sz)
    outs = [((sz.rows, sz.width), F4)] + [saved[k] for k in SAVED]
    res = pl.pallas_call(
        functools.partial(first_kernel, sz),
        grid_spec=pltpu.PrefetchScalarGridSpec(
            num_scalar_prefetch=1,
            grid=(sz.images,),
            in_specs=[image_spec(tokens.shape[1:])] + [spec_any()] * 6,
            out_specs=[image_spec(shape) for shape, _ in outs],
            scratch_shapes=weight_scratch(sz, BF)
            + load_scratch(sz)
            + [pltpu.VMEM((sz.rows, sz.width), F4)]
            + scratch_of(local_shapes(sz), ("vt", "ct")),
        ),
        out_shape=[jax.ShapeDtypeStruct((sz.images,) + tuple(a), b) for a, b in outs],
        compiler_params=params(),
        name="first",
    )(tab, tokens, *halves)
    return res[0], list(res[1:])


def run_second(sz, tab, x1, cot, halves):
    res = pl.pallas_call(
        functools.partial(second_kernel, sz),
        grid_spec=pltpu.PrefetchScalarGridSpec(
            num_scalar_prefetch=1,
            grid=(sz.images,),
            in_specs=[image_spec(x1.shape[1:]), image_spec(cot.shape[1:])] + [spec_any()] * 6,
            out_specs=[image_spec(cot.shape[1:]), image_spec(x1.shape[1:])] + [spec_any()] * 6,
            scratch_shapes=weight_scratch(sz, BF)
            + weight_scratch(sz, F4)
            + load_scratch(sz)
            + [pltpu.VMEM((sz.rows, sz.width), F4)]
            + scratch_of(saved_shapes(sz), SAVED)
            + scratch_of(local_shapes(sz), ("vt", "ct"))
            + scratch_of(temp_shapes(sz), TEMPS),
        ),
        out_shape=[
            jax.ShapeDtypeStruct(cot.shape, F4),
            jax.ShapeDtypeStruct(x1.shape, F4),
        ]
        + packed_outs(sz),
        compiler_params=params(),
        name="second",
    )(tab, x1, cot, *halves)
    return res[0], res[1], list(res[2:])


def run_third(sz, tab, dx, saved, halves):
    shape = (sz.images, sz.seq, sz.width)
    res = pl.pallas_call(
        functools.partial(third_kernel, sz),
        grid_spec=pltpu.PrefetchScalarGridSpec(
            num_scalar_prefetch=1,
            grid=(sz.images,),
            in_specs=[image_spec(dx.shape[1:])]
            + [image_spec(a.shape[1:]) for a in saved]
            + [spec_any()] * 6,
            out_specs=[image_spec(shape[1:])] + [spec_any()] * 6,
            scratch_shapes=weight_scratch(sz, BF)
            + weight_scratch(sz, F4)
            + load_scratch(sz)
            + scratch_of(temp_shapes(sz), TEMPS),
        ),
        out_shape=[jax.ShapeDtypeStruct(shape, F4)] + packed_outs(sz),
        compiler_params=params(),
        name="third",
    )(tab, dx, *saved, *halves)
    return res[0], list(res[1:])


def adam_math(grad_sum, weight, first, second, count_rows, decay_on):
    grad = grad_sum / count_rows
    first_new = BETA_ONE * first + (1.0 - BETA_ONE) * grad
    second_new = BETA_TWO * second + (1.0 - BETA_TWO) * grad * grad
    fix_one = 1.0 - BETA_ONE**STEP
    fix_two = 1.0 - BETA_TWO**STEP
    direction = first_new / fix_one / (jnp.sqrt(second_new / fix_two) + ADAM_EPS)
    if decay_on:
        direction = direction + DECAY * weight
    return (grad, weight - LEARN_RATE * direction, first_new, second_new)


def adam_kernel(sz, count_rows, *refs):
    refs = list(refs)
    take = lambda k: [refs.pop(0) for _ in range(k)]
    sums = [take(6) for _ in range(sz.layers)]
    state = [take(7) for _ in range(3)]
    outs = [take(7) for _ in range(4)]
    (st,) = take(1)

    def put(i, index, grad):
        vals = adam_math(grad, *(state[k][i][index] for k in range(3)), count_rows, i >= 3)
        for k in range(4):
            outs[k][i][index] = vals[k]

    for layer in range(sz.layers):
        for p, (first, count) in enumerate(sz.parts):
            a, b = sums[layer][2 * p : 2 * p + 2]
            st[first : first + count, :] = a[0].astype(F4) + b[0].astype(F4)
        s = sz.small
        put(0, layer, st[s : s + 2, 0 : sz.kr])
        put(1, layer, st[s + 2 : s + 8, 0 : sz.kr])
        put(2, (slice(layer, layer + 1), slice(None)), st[s : s + 1, 64 : 64 + sz.ku])
        for i, (name, blocks, rows, at) in enumerate(sz.segs):
            for c in range(blocks):
                index = (layer, slice(None), slice(c * LANES, (c + 1) * LANES))
                put(3 + i, index, st[at + c * rows : at + (c + 1) * rows, :])


def run_adam(sz, sums, params_, firsts, seconds, count_rows):
    shapes = [jax.ShapeDtypeStruct(p.shape, F4) for p in params_]
    res = pl.pallas_call(
        functools.partial(adam_kernel, sz, count_rows),
        out_shape=shapes * 4,
        scratch_shapes=[pltpu.VMEM((sz.pack, LANES), F4)],
        compiler_params=pltpu.CompilerParams(vmem_limit_bytes=VMEM_LIMIT),
        name="adam",
    )(*[x for layer in sums for x in layer], *params_, *firsts, *seconds)
    return res


def body(tokens, counts, cotangent, *state):
    params_, firsts, seconds = state[0:7], state[7:14], state[14:21]
    groups, _, seq, width = tokens.shape
    images = 2 * groups
    n = lax.axis_size("dp")
    layers, hidden = params_[3].shape[0], params_[5].shape[2]
    sz = Sizes(n, images, seq, width, hidden, layers)

    me = lax.axis_index("dp")
    table = []
    for p in range(3):
        place = np.asarray(sz.place(p), np.int32)
        mine = sum(((me >> (b.bit_length() - 1)) & 1) << s for s, b in enumerate(sz.orders[p]))
        table.append(jnp.bitwise_xor(jnp.asarray(place), mine.astype(jnp.int32)))
    live = jnp.stack([jnp.ones_like(counts), (counts == 2).astype(jnp.int32)], axis=1)
    tab = jnp.concatenate(table + [live.reshape(-1)])

    packed = pack_params(sz, params_)
    halves = [gather_parts(sz, packed[layer]) for layer in range(layers)]
    x1, saved = run_first(sz, tab, tokens.reshape(images, seq, width), halves[0])
    out, dx, grads_one = run_second(
        sz, tab, x1, cotangent.reshape(images, seq, width), halves[1]
    )
    sums_one = scatter_parts(sz, grads_one)
    input_grad, grads_zero = run_third(sz, tab, dx, saved, halves[0])
    sums_zero = scatter_parts(sz, grads_zero)
    res = run_adam(sz, [sums_zero, sums_one], params_, firsts, seconds, float(n * images * seq))
    return (out.reshape(tokens.shape), input_grad.reshape(tokens.shape), *res)


def solution(mesh):
    tok = P("dp", None, None, None)
    state = [P(None, None, "dp")] * 2 + [P(None, "dp")] + [P(None, "dp", None)] * 4
    return jax.shard_map(
        body,
        mesh=mesh,
        in_specs=(tok, P("dp"), tok, *(state * 3)),
        out_specs=(tok, tok, *(state * 4)),
        check_vma=False,
    )
```

time: 1320 us -> 376 us (0.28); the launches traced: 1310 us -> 379 us
  blocking collectives: 544 us -> 0 us
  matrix products: 252 us -> 0 us
  local copies, waits for them, and re-layouts: 267 us -> 57.8 us
  Pallas kernels: 0 us -> 204 us
  other arithmetic: 100 us -> 8.28 us
  starting transfers between devices: 124 us -> 84.9 us
  waiting for transfers between devices: 2.74 us -> 22.4 us
  between operations: 16.9 us -> 1.52 us
    all_gather x8 -> x0, blocking collectives: 326 us -> none  [the longest x2 88 us: fetch_layer(): lax.all_gather(qkv_part, 'dp', axis=0, tiled=True)]
    dot_general x36 -> x0, matrix products: 252 us -> none  [the longest x12 92.3 us: mixed(): return jnp.einsum(form, left, right, preferred_element_type=jnp.float32)]
    unnamed x3 -> x0, blocking collectives: 218 us -> none
    pallas_call x0 -> x5, Pallas kernels: none -> 204 us  [the longest x1 89.7 us: run_second(): pl.pallas_call(functools.partial(second_kernel, sz), grid_spec=pltpu.Pref...]
    reshape x26 -> x2, local copies, waits for them, and re-layouts: 142 us -> 0.17 us  [body(): tab = jnp.concatenate(table + [live.reshape(-1)])]
    unnamed x48 -> x0, starting transfers between devices: 124 us -> none
    ppermute x0 -> x60, starting transfers between devices: none -> 84.9 us  [swap(): return lax.ppermute(x, 'dp', [(i, i ^ bit) for i in range(n)])]
    reduce_sum x15 -> x0, other arithmetic: 59 us -> none  [the longest x4 19.3 us: normalize(): jnp.mean(center * center, axis=-1, keepdims=True) + NORM_EPS]
  transfers between devices with their start and end apart: 54 -> 60, of which waited for: 1 -> 11; matrix products, arithmetic and copies ran while one was open for 28% -> 9% of each run, Pallas kernels for 0% -> 29%
where the time goes in v1:
time: 376 us; the launch traced here: 379 us
  Pallas kernels  204 us (54%)
  starting transfers between devices  84.9 us (23%)
  local copies, waits for them, and re-layouts  57.8 us (15%)
  waiting for transfers between devices  22.4 us (6%)
  other arithmetic  8.28 us (2%)
    pallas_call x1, Pallas kernels, run_second(): pl.pallas_call(functools.partial(second_kernel, sz), grid_spec=pltpu.Pref...  89.7 us
    ppermute x60, starting transfers between devices, swap(): return lax.ppermute(x, 'dp', [(i, i ^ bit) for i in range(n)])  84.9 us
    pallas_call x1, Pallas kernels, run_third(): pl.pallas_call(functools.partial(third_kernel, sz), grid_spec=pltpu.Prefe...  62.7 us
    unnamed x131, local copies, waits for them, and re-layouts  55.3 us
    pallas_call x1, Pallas kernels, run_first(): pl.pallas_call(functools.partial(first_kernel, sz), grid_spec=pltpu.Prefe...  46.7 us
    ppermute x60, waiting for transfers between devices, swap(): return lax.ppermute(x, 'dp', [(i, i ^ bit) for i in range(n)])  22.4 us
  transfers between devices with their start and end apart: 60, of which 11 were waited for; matrix products, arithmetic and copies ran while one was open for 9% of the time, Pallas kernels for 29%

profile of v1, /device:TPU:0, one launch (start us, length us, event | category | flops | bytes accessed | tf_op | source)
XLA Modules:
  0.0 379.2 jit_solution(13635097286385283458)
XLA Ops:
  0.7 1.6 copy.99.wu.refs_17_
  2.3 1.6 copy.97.wq.refs_15_
  6.5 1.9 pack.1
  8.4 4.1 %collective-permute-start.10 = (bf16[1,136,128]{2,1,0:T(8,128)(2,1)}, bf16[1,136,128]{2,1,0:T(8,128)(2,1)S(1)}, u32[]{:S(2)}, u32[]{:S(2)}) collective-permute-start(bf16[1,136,128]{2,1,0:T(8,128)(2,1)} %bitcast.42), channel_id=1, source_target_pairs={{0,16},{1,17},{2,18},{3,19},{4,20},{5,21},{6,22},{7,23},{8,24},{9,... | collective-permute-start | bytes 104456 | tf_op jit(solution)/shard_map/ppermute | solution.py:143
  12.5 2.9 collective-permute-start
  15.4 2.9 collective-permute-start.20
  22.2 3.1 copy.95
  25.3 2.0 copy.100
  27.5 4.7 %collective-permute-done.25 = bf16[1,136,128]{2,1,0:T(8,128)(2,1)S(1)} collective-permute-done((bf16[1,136,128]{2,1,0:T(8,128)(2,1)S(1)}, bf16[1,136,128]{2,1,0:T(8,128)(2,1)S(1)}, u32[]{:S(2)}, u32[]{:S(2)}) %collective-permute-start.25) | collective-permute-done | bytes 34848 | tf_op jit(solution)/shard_map/ppermute | solution.py:143
  34.9 1.6 collective-permute-start.6
  36.5 1.6 collective-permute-start.1
  39.4 1.6 collective-permute-start.12
  42.2 1.6 collective-permute-start.7
  43.8 1.6 collective-permute-start.2
  46.8 1.6 collective-permute-start.13
  50.8 1.6 collective-permute-start.8
  52.4 1.7 collective-permute-done.17
  54.7 1.6 collective-permute-start.18
  57.7 1.6 collective-permute-start.23
  61.1 3.3 collective-permute-done.18
  69.9 46.7 %first.1 = (f32[12,208,384]{2,1,0:T(8,128)}, f32[12,208,384]{2,1,0:T(8,128)}, f32[12,208,1]{2,1,0:T(8,128)}, bf16[12,208,384]{2,1,0:T(8,128)(2,1)}, bf16[12,208,...) custom-call(s32[108]{0:T(128)} %pad_add_fusion.tab, ...), custom_call_target="tpu_custom_call" | custom-call | tf_op jit(solution)/shard_map/first/pallas_call | solution.py:572
  116.6 89.7 %second.1 = (f32[12,197,384]{2,1,0:T(8,128)}, f32[12,208,384]{2,1,0:T(8,128)}, bf16[16,152,128]{2,1,0:T(8,128)(2,1)}, bf16[16,152,128]{2,1,0:T(8,128)(2,1)}, bf1...) custom-call(s32[108]{0:T(128)} %pad_add_fusion.tab, ...), custom_call_target="tpu_custom_call" | custom-call | tf_op jit(solution)/shard_map/second/pallas_call | solution.py:592
  206.4 62.7 %third.1 = (f32[12,197,384]{2,1,0:T(8,128)}, bf16[16,152,128]{2,1,0:T(8,128)(2,1)}, bf16[16,152,128]{2,1,0:T(8,128)(2,1)}, bf16[16,152,128]{2,1,0:T(8,128)(2,1)}...) custom-call(s32[108]{0:T(128)} %pad_add_fusion.tab, ...), custom_call_target="tpu_custom_call" | custom-call | tf_op jit(solution)/shard_map/third/pallas_call | solution.py:620
  271.5 1.6 collective-permute-start.56
  274.9 1.7 collective-permute-start.51
  276.6 18.5 %collective-permute-start.46 = (bf16[8,152,128]{2,1,0:T(8,128)(2,1)S(1)}, bf16[8,152,128]{2,1,0:T(8,128)(2,1)S(1)}, u32[]{:S(2)}, u32[]{:S(2)}) collective-permute-start(bf16[8,152,128]{2,1,0:T(8,128)(2,1)S(1)} %get-tuple-element.219), channel_id=1, source_target_pairs={{0,2},{1,3},{2,0},{3,1},{4,6},{5,7},{6,4},{7,5},{8,10},{9,11},{10,... | collective-permute-start | bytes 933896 | tf_op jit(solution)/shard_map/ppermute | solution.py:143
  295.5 5.7 %collective-permute-start.57 = (bf16[4,136,128]{2,1,0:T(8,128)(2,1)S(1)}, bf16[4,136,128]{2,1,0:T(8,128)(2,1)S(1)}, u32[]{:S(2)}, u32[]{:S(2)}) collective-permute-start(bf16[4,136,128]{2,1,0:T(8,128)(2,1)S(1)} %get-tuple-element.237), channel_id=1, source_target_pairs={{0,8},{1,9},{2,10},{3,11},{4,12},{5,13},{6,14},{7,15},{8,0},{9,1},... | collective-permute-start | bytes 417800 | tf_op jit(solution)/shard_map/ppermute | solution.py:143
  301.4 2.0 collective-permute-done.46
  303.4 3.4 collective-permute-start.52
  306.8 1.8 collective-permute-start.47
  310.0 2.0 collective-permute-start.37
  312.1 2.1 collective-permute-start.32
  315.0 3.6 collective-permute-done.58
  321.2 1.8 collective-permute-start.53
  327.5 2.5 collective-permute-start.54
  331.7 2.5 collective-permute-start.39
  335.9 2.5 collective-permute-start.44
  343.7 3.7 copy.114
  347.4 3.7 copy.113
  351.8 3.3 adam.1
  355.0 1.7 copy.118
  356.7 1.7 copy.122
  358.4 1.7 copy.126
  360.1 1.7 copy.130
  361.8 1.6 copy.116
  363.4 1.6 copy.120
  365.1 1.6 copy.124
  366.7 1.6 copy.128
  (263 shorter events, 59.1 us)
Async XLA Ops:
  8.4 19.0 %collective-permute-start.10 = (bf16[1,136,128]{2,1,0:T(8,128)(2,1)}, bf16[1,136,128]{2,1,0:T(8,128)(2,1)S(1)}, u32[]{:S(2)}, u32[]{:S(2)}) collective-permute-start(bf16[1,136,128]{2,1,0:T(8,128)(2,1)} %bitcast.42), channel_id=1, source_target_pairs={{0,16},{1,17},{2,18},{3,19},{4,20},{5,21},{6,22},{7,23},{8,24},{9,... | collective-permute-start | bytes 104456 | tf_op jit(solution)/shard_map/ppermute | solution.py:143
  12.5 21.9 %collective-permute-start.5 = (bf16[1,152,128]{2,1,0:T(8,128)(2,1)}, bf16[1,152,128]{2,1,0:T(8,128)(2,1)S(1)}, u32[]{:S(2)}, u32[]{:S(2)}) collective-permute-start(bf16[1,152,128]{2,1,0:T(8,128)(2,1)} %bitcast.34), channel_id=1, source_target_pairs={{0,16},{1,17},{2,18},{3,19},{4,20},{5,21},{6,22},{7,23},{8,24},{9,... | collective-permute-start | bytes 116744 | tf_op jit(solution)/shard_map/ppermute | solution.py:143
  12.5 22.4 %collective-permute-start = (bf16[1,152,128]{2,1,0:T(8,128)(2,1)}, bf16[1,152,128]{2,1,0:T(8,128)(2,1)S(1)}, u32[]{:S(2)}, u32[]{:S(2)}) collective-permute-start(bf16[1,152,128]{2,1,0:T(8,128)(2,1)} %bitcast.30), channel_id=1, source_target_pairs={{0,16},{1,17},{2,18},{3,19},{4,20},{5,21},{6,22},{7,23},{8,24},{9,... | collective-permute-start | bytes 116744 | tf_op jit(solution)/shard_map/ppermute | solution.py:143
  15.4 21.2 %collective-permute-start.15 = (bf16[1,152,128]{2,1,0:T(8,128)(2,1)}, bf16[1,152,128]{2,1,0:T(8,128)(2,1)S(1)}, u32[]{:S(2)}, u32[]{:S(2)}) collective-permute-start(bf16[1,152,128]{2,1,0:T(8,128)(2,1)} %bitcast.26), channel_id=1, source_target_pairs={{0,16},{1,17},{2,18},{3,19},{4,20},{5,21},{6,22},{7,23},{8,24},{9,... | collective-permute-start | bytes 116744 | tf_op jit(solution)/shard_map/ppermute | solution.py:143
  15.4 22.8 %collective-permute-start.20 = (bf16[1,152,128]{2,1,0:T(8,128)(2,1)}, bf16[1,152,128]{2,1,0:T(8,128)(2,1)S(1)}, u32[]{:S(2)}, u32[]{:S(2)}) collective-permute-start(bf16[1,152,128]{2,1,0:T(8,128)(2,1)} %bitcast.22), channel_id=1, source_target_pairs={{0,16},{1,17},{2,18},{3,19},{4,20},{5,21},{6,22},{7,23},{8,24},{9,... | collective-permute-start | bytes 116744 | tf_op jit(solution)/shard_map/ppermute | solution.py:143
  32.2 6.6 %collective-permute-start.11 = (bf16[2,136,128]{2,1,0:T(8,128)(2,1)S(1)}, bf16[2,136,128]{2,1,0:T(8,128)(2,1)S(1)}, u32[]{:S(2)}, u32[]{:S(2)}) collective-permute-start(bf16[2,136,128]{2,1,0:T(8,128)(2,1)S(1)} %pad_maximum_fusion.16), channel_id=1, source_target_pairs={{0,2},{1,3},{2,0},{3,1},{4,6},{5,7},{6,4},{7,5},{8,10},{9,11},{10,... | collective-permute-start | bytes 208904 | tf_op jit(solution)/shard_map/ppermute | solution.py:143
  34.9 6.8 %collective-permute-start.6 = (bf16[2,152,128]{2,1,0:T(8,128)(2,1)S(1)}, bf16[2,152,128]{2,1,0:T(8,128)(2,1)S(1)}, u32[]{:S(2)}, u32[]{:S(2)}) collective-permute-start(bf16[2,152,128]{2,1,0:T(8,128)(2,1)S(1)} %pad_maximum_fusion.13), channel_id=1, source_target_pairs={{0,4},{1,5},{2,6},{3,7},{4,0},{5,1},{6,2},{7,3},{8,12},{9,13},{10,... | collective-permute-start | bytes 233480 | tf_op jit(solution)/shard_map/ppermute | solution.py:143
  38.8 6.7 %collective-permute-start.21 = (bf16[2,152,128]{2,1,0:T(8,128)(2,1)S(1)}, bf16[2,152,128]{2,1,0:T(8,128)(2,1)S(1)}, u32[]{:S(2)}, u32[]{:S(2)}) collective-permute-start(bf16[2,152,128]{2,1,0:T(8,128)(2,1)S(1)} %pad_maximum_fusion.15), channel_id=1, source_target_pairs={{0,4},{1,5},{2,6},{3,7},{4,0},{5,1},{6,2},{7,3},{8,12},{9,13},{10,... | collective-permute-start | bytes 233480 | tf_op jit(solution)/shard_map/ppermute | solution.py:143
  39.4 6.7 %collective-permute-start.12 = (bf16[4,136,128]{2,1,0:T(8,128)(2,1)S(1)}, bf16[4,136,128]{2,1,0:T(8,128)(2,1)S(1)}, u32[]{:S(2)}, u32[]{:S(2)}) collective-permute-start(bf16[4,136,128]{2,1,0:T(8,128)(2,1)S(1)} %pad_maximum_fusion.10), channel_id=1, source_target_pairs={{0,8},{1,9},{2,10},{3,11},{4,12},{5,13},{6,14},{7,15},{8,0},{9,1},... | collective-permute-start | bytes 417800 | tf_op jit(solution)/shard_map/ppermute | solution.py:143
  42.2 6.9 %collective-permute-start.7 = (bf16[4,152,128]{2,1,0:T(8,128)(2,1)S(1)}, bf16[4,152,128]{2,1,0:T(8,128)(2,1)S(1)}, u32[]{:S(2)}, u32[]{:S(2)}) collective-permute-start(bf16[4,152,128]{2,1,0:T(8,128)(2,1)S(1)} %pad_maximum_fusion.7), channel_id=1, source_target_pairs={{0,2},{1,3},{2,0},{3,1},{4,6},{5,7},{6,4},{7,5},{8,10},{9,11},{10,... | collective-permute-start | bytes 466952 | tf_op jit(solution)/shard_map/ppermute | solution.py:143
  43.8 7.0 %collective-permute-start.2 = (bf16[4,152,128]{2,1,0:T(8,128)(2,1)S(1)}, bf16[4,152,128]{2,1,0:T(8,128)(2,1)S(1)}, u32[]{:S(2)}, u32[]{:S(2)}) collective-permute-start(bf16[4,152,128]{2,1,0:T(8,128)(2,1)S(1)} %pad_maximum_fusion.6), channel_id=1, source_target_pairs={{0,4},{1,5},{2,6},{3,7},{4,0},{5,1},{6,2},{7,3},{8,12},{9,13},{10,... | collective-permute-start | bytes 466952 | tf_op jit(solution)/shard_map/ppermute | solution.py:143
  45.4 8.7 %collective-permute-start.17 = (bf16[4,152,128]{2,1,0:T(8,128)(2,1)S(1)}, bf16[4,152,128]{2,1,0:T(8,128)(2,1)S(1)}, u32[]{:S(2)}, u32[]{:S(2)}) collective-permute-start(bf16[4,152,128]{2,1,0:T(8,128)(2,1)S(1)} %pad_maximum_fusion.8), channel_id=1, source_target_pairs={{0,4},{1,5},{2,6},{3,7},{4,0},{5,1},{6,2},{7,3},{8,12},{9,13},{10,... | collective-permute-start | bytes 466952 | tf_op jit(solution)/shard_map/ppermute | solution.py:143
  46.1 8.6 %collective-permute-start.22 = (bf16[4,152,128]{2,1,0:T(8,128)(2,1)S(1)}, bf16[4,152,128]{2,1,0:T(8,128)(2,1)S(1)}, u32[]{:S(2)}, u32[]{:S(2)}) collective-permute-start(bf16[4,152,128]{2,1,0:T(8,128)(2,1)S(1)} %pad_maximum_fusion.9), channel_id=1, source_target_pairs={{0,2},{1,3},{2,0},{3,1},{4,6},{5,7},{6,4},{7,5},{8,10},{9,11},{10,... | collective-permute-start | bytes 466952 | tf_op jit(solution)/shard_map/ppermute | solution.py:143
  46.8 10.9 %collective-permute-start.13 = (bf16[8,136,128]{2,1,0:T(8,128)(2,1)S(1)}, bf16[8,136,128]{2,1,0:T(8,128)(2,1)S(1)}, u32[]{:S(2)}, u32[]{:S(2)}) collective-permute-start(bf16[8,136,128]{2,1,0:T(8,128)(2,1)S(1)} %pad_maximum_fusion.4), channel_id=1, source_target_pairs={{0,4},{1,5},{2,6},{3,7},{4,0},{5,1},{6,2},{7,3},{8,12},{9,13},{10,... | collective-permute-start | bytes 835592 | tf_op jit(solution)/shard_map/ppermute | solution.py:143
  49.1 17.3 %collective-permute-start.28 = (bf16[8,136,128]{2,1,0:T(8,128)(2,1)S(1)}, bf16[8,136,128]{2,1,0:T(8,128)(2,1)S(1)}, u32[]{:S(2)}, u32[]{:S(2)}) collective-permute-start(bf16[8,136,128]{2,1,0:T(8,128)(2,1)S(1)} %pad_maximum_fusion.5), channel_id=1, source_target_pairs={{0,4},{1,5},{2,6},{3,7},{4,0},{5,1},{6,2},{7,3},{8,12},{9,13},{10,... | collective-permute-start | bytes 835592 | tf_op jit(solution)/shard_map/ppermute | solution.py:143
  50.8 8.6 %collective-permute-start.8 = (bf16[8,152,128]{2,1,0:T(8,128)(2,1)S(1)}, bf16[8,152,128]{2,1,0:T(8,128)(2,1)S(1)}, u32[]{:S(2)}, u32[]{:S(2)}) collective-permute-start(bf16[8,152,128]{2,1,0:T(8,128)(2,1)S(1)} %pad_maximum_fusion.1), channel_id=1, source_target_pairs={{0,8},{1,9},{2,10},{3,11},{4,12},{5,13},{6,14},{7,15},{8,0},{9,1},... | collective-permute-start | bytes 933896 | tf_op jit(solution)/shard_map/ppermute | solution.py:143
  54.1 6.9 %collective-permute-start.3 = (bf16[8,152,128]{2,1,0:T(8,128)(2,1)S(1)}, bf16[8,152,128]{2,1,0:T(8,128)(2,1)S(1)}, u32[]{:S(2)}, u32[]{:S(2)}) collective-permute-start(bf16[8,152,128]{2,1,0:T(8,128)(2,1)S(1)} %pad_maximum_fusion), channel_id=1, source_target_pairs={{0,2},{1,3},{2,0},{3,1},{4,6},{5,7},{6,4},{7,5},{8,10},{9,11},{10,... | collective-permute-start | bytes 933896 | tf_op jit(solution)/shard_map/ppermute | solution.py:143
  54.7 9.7 %collective-permute-start.18 = (bf16[8,152,128]{2,1,0:T(8,128)(2,1)S(1)}, bf16[8,152,128]{2,1,0:T(8,128)(2,1)S(1)}, u32[]{:S(2)}, u32[]{:S(2)}) collective-permute-start(bf16[8,152,128]{2,1,0:T(8,128)(2,1)S(1)} %pad_maximum_fusion.2), channel_id=1, source_target_pairs={{0,2},{1,3},{2,0},{3,1},{4,6},{5,7},{6,4},{7,5},{8,10},{9,11},{10,... | collective-permute-start | bytes 933896 | tf_op jit(solution)/shard_map/ppermute | solution.py:143
  57.7 7.4 %collective-permute-start.23 = (bf16[8,152,128]{2,1,0:T(8,128)(2,1)S(1)}, bf16[8,152,128]{2,1,0:T(8,128)(2,1)S(1)}, u32[]{:S(2)}, u32[]{:S(2)}) collective-permute-start(bf16[8,152,128]{2,1,0:T(8,128)(2,1)S(1)} %pad_maximum_fusion.3), channel_id=1, source_target_pairs={{0,8},{1,9},{2,10},{3,11},{4,12},{5,13},{6,14},{7,15},{8,0},{9,1},... | collective-permute-start | bytes 933896 | tf_op jit(solution)/shard_map/ppermute | solution.py:143
  59.3 7.7 %collective-permute-start.14 = (bf16[16,136,128]{2,1,0:T(8,128)(2,1)S(1)}, bf16[16,136,128]{2,1,0:T(8,128)(2,1)S(1)}, u32[]{:S(2)}, u32[]{:S(2)}) collective-permute-start(bf16[16,136,128]{2,1,0:T(8,128)(2,1)S(1)} %constant_dynamic-update-slice_fusion.10.refs_4_.refs_17_), channel_id=1, source_target_pairs={{0,1},{1,0},{2,3},{3,2},{4,5},{5,4},{6,7},{7,6},{8,9},{9,8},{10,11... | collective-permute-start | bytes 1671176 | tf_op jit(solution)/shard_map/ppermute | solution.py:143
  61.0 7.2 %collective-permute-start.9 = (bf16[16,152,128]{2,1,0:T(8,128)(2,1)S(1)}, bf16[16,152,128]{2,1,0:T(8,128)(2,1)S(1)}, u32[]{:S(2)}, u32[]{:S(2)}) collective-permute-start(bf16[16,152,128]{2,1,0:T(8,128)(2,1)S(1)} %constant_dynamic-update-slice_fusion.5.refs_2_.refs_15_), channel_id=1, source_target_pairs={{0,1},{1,0},{2,3},{3,2},{4,5},{5,4},{6,7},{7,6},{8,9},{9,8},{10,11... | collective-permute-start | bytes 1867784 | tf_op jit(solution)/shard_map/ppermute | solution.py:143
  65.1 51.5 %collective-permute-start.19 = (bf16[16,152,128]{2,1,0:T(8,128)(2,1)}, bf16[16,152,128]{2,1,0:T(8,128)(2,1)}, u32[]{:S(2)}, u32[]{:S(2)}) collective-permute-start(bf16[16,152,128]{2,1,0:T(8,128)(2,1)} %constant_dynamic-update-slice_fusion.15.refs_0_), channel_id=1, source_target_pairs={{0,1},{1,0},{2,3},{3,2},{4,5},{5,4},{6,7},{7,6},{8,9},{9,8},{10,11... | collective-permute-start | bytes 1867784 | tf_op jit(solution)/shard_map/ppermute | solution.py:143
  66.3 50.3 %collective-permute-start.24 = (bf16[16,152,128]{2,1,0:T(8,128)(2,1)}, bf16[16,152,128]{2,1,0:T(8,128)(2,1)}, u32[]{:S(2)}, u32[]{:S(2)}) collective-permute-start(bf16[16,152,128]{2,1,0:T(8,128)(2,1)} %constant_dynamic-update-slice_fusion.20.refs_2_), channel_id=1, source_target_pairs={{0,1},{1,0},{2,3},{3,2},{4,5},{5,4},{6,7},{7,6},{8,9},{9,8},{10,11... | collective-permute-start | bytes 1867784 | tf_op jit(solution)/shard_map/ppermute | solution.py:143
  67.1 49.5 %collective-permute-start.29 = (bf16[16,136,128]{2,1,0:T(8,128)(2,1)}, bf16[16,136,128]{2,1,0:T(8,128)(2,1)}, u32[]{:S(2)}, u32[]{:S(2)}) collective-permute-start(bf16[16,136,128]{2,1,0:T(8,128)(2,1)} %constant_dynamic-update-slice_fusion.25.refs_4_), channel_id=1, source_target_pairs={{0,1},{1,0},{2,3},{3,2},{4,5},{5,4},{6,7},{7,6},{8,9},{9,8},{10,11... | collective-permute-start | bytes 1671176 | tf_op jit(solution)/shard_map/ppermute | solution.py:143
  206.3 63.9 %collective-permute-start.55 = (bf16[16,136,128]{2,1,0:T(8,128)(2,1)}, bf16[16,136,128]{2,1,0:T(8,128)(2,1)}, u32[]{:S(2)}, u32[]{:S(2)}) collective-permute-start(bf16[16,136,128]{2,1,0:T(8,128)(2,1)} %get-tuple-element.127), channel_id=1, source_target_pairs={{0,1},{1,0},{2,3},{3,2},{4,5},{5,4},{6,7},{7,6},{8,9},{9,8},{10,11... | collective-permute-start | bytes 1671176 | tf_op jit(solution)/shard_map/ppermute | solution.py:143
  269.8 6.8 %collective-permute-start.35 = (bf16[16,152,128]{2,1,0:T(8,128)(2,1)}, bf16[16,152,128]{2,1,0:T(8,128)(2,1)S(1)}, u32[]{:S(2)}, u32[]{:S(2)}) collective-permute-start(bf16[16,152,128]{2,1,0:T(8,128)(2,1)} %get-tuple-element.119), channel_id=1, source_target_pairs={{0,1},{1,0},{2,3},{3,2},{4,5},{5,4},{6,7},{7,6},{8,9},{9,8},{10,11... | collective-permute-start | bytes 1867784 | tf_op jit(solution)/shard_map/ppermute | solution.py:143
  270.3 25.0 %collective-permute-start.30 = (bf16[16,152,128]{2,1,0:T(8,128)(2,1)}, bf16[16,152,128]{2,1,0:T(8,128)(2,1)S(1)}, u32[]{:S(2)}, u32[]{:S(2)}) collective-permute-start(bf16[16,152,128]{2,1,0:T(8,128)(2,1)} %get-tuple-element.117), channel_id=1, source_target_pairs={{0,1},{1,0},{2,3},{3,2},{4,5},{5,4},{6,7},{7,6},{8,9},{9,8},{10,11... | collective-permute-start | bytes 1867784 | tf_op jit(solution)/shard_map/ppermute | solution.py:143
  271.5 23.9 %collective-permute-start.56 = (bf16[8,136,128]{2,1,0:T(8,128)(2,1)S(1)}, bf16[8,136,128]{2,1,0:T(8,128)(2,1)S(1)}, u32[]{:S(2)}, u32[]{:S(2)}) collective-permute-start(bf16[8,136,128]{2,1,0:T(8,128)(2,1)S(1)} %get-tuple-element.225), channel_id=1, source_target_pairs={{0,4},{1,5},{2,6},{3,7},{4,0},{5,1},{6,2},{7,3},{8,12},{9,13},{10,... | collective-permute-start | bytes 835592 | tf_op jit(solution)/shard_map/ppermute | solution.py:143
  274.2 21.3 %collective-permute-start.41 = (bf16[8,136,128]{2,1,0:T(8,128)(2,1)S(1)}, bf16[8,136,128]{2,1,0:T(8,128)(2,1)S(1)}, u32[]{:S(2)}, u32[]{:S(2)}) collective-permute-start(bf16[8,136,128]{2,1,0:T(8,128)(2,1)S(1)} %get-tuple-element.227), channel_id=1, source_target_pairs={{0,4},{1,5},{2,6},{3,7},{4,0},{5,1},{6,2},{7,3},{8,12},{9,13},{10,... | collective-permute-start | bytes 835592 | tf_op jit(solution)/shard_map/ppermute | solution.py:143
  274.9 26.4 %collective-permute-start.51 = (bf16[8,152,128]{2,1,0:T(8,128)(2,1)S(1)}, bf16[8,152,128]{2,1,0:T(8,128)(2,1)S(1)}, u32[]{:S(2)}, u32[]{:S(2)}) collective-permute-start(bf16[8,152,128]{2,1,0:T(8,128)(2,1)S(1)} %get-tuple-element.217), channel_id=1, source_target_pairs={{0,8},{1,9},{2,10},{3,11},{4,12},{5,13},{6,14},{7,15},{8,0},{9,1},... | collective-permute-start | bytes 933896 | tf_op jit(solution)/shard_map/ppermute | solution.py:143
  276.6 26.7 %collective-permute-start.46 = (bf16[8,152,128]{2,1,0:T(8,128)(2,1)S(1)}, bf16[8,152,128]{2,1,0:T(8,128)(2,1)S(1)}, u32[]{:S(2)}, u32[]{:S(2)}) collective-permute-start(bf16[8,152,128]{2,1,0:T(8,128)(2,1)S(1)} %get-tuple-element.219), channel_id=1, source_target_pairs={{0,2},{1,3},{2,0},{3,1},{4,6},{5,7},{6,4},{7,5},{8,10},{9,11},{10,... | collective-permute-start | bytes 933896 | tf_op jit(solution)/shard_map/ppermute | solution.py:143
  295.2 11.6 %collective-permute-start.36 = (bf16[8,152,128]{2,1,0:T(8,128)(2,1)S(1)}, bf16[8,152,128]{2,1,0:T(8,128)(2,1)S(1)}, u32[]{:S(2)}, u32[]{:S(2)}) collective-permute-start(bf16[8,152,128]{2,1,0:T(8,128)(2,1)S(1)} %get-tuple-element.221), channel_id=1, source_target_pairs={{0,8},{1,9},{2,10},{3,11},{4,12},{5,13},{6,14},{7,15},{8,0},{9,1},... | collective-permute-start | bytes 933896 | tf_op jit(solution)/shard_map/ppermute | solution.py:143
  295.4 14.6 %collective-permute-start.31 = (bf16[8,152,128]{2,1,0:T(8,128)(2,1)S(1)}, bf16[8,152,128]{2,1,0:T(8,128)(2,1)S(1)}, u32[]{:S(2)}, u32[]{:S(2)}) collective-permute-start(bf16[8,152,128]{2,1,0:T(8,128)(2,1)S(1)} %get-tuple-element.223), channel_id=1, source_target_pairs={{0,2},{1,3},{2,0},{3,1},{4,6},{5,7},{6,4},{7,5},{8,10},{9,11},{10,... | collective-permute-start | bytes 933896 | tf_op jit(solution)/shard_map/ppermute | solution.py:143
  295.5 16.6 %collective-permute-start.57 = (bf16[4,136,128]{2,1,0:T(8,128)(2,1)S(1)}, bf16[4,136,128]{2,1,0:T(8,128)(2,1)S(1)}, u32[]{:S(2)}, u32[]{:S(2)}) collective-permute-start(bf16[4,136,128]{2,1,0:T(8,128)(2,1)S(1)} %get-tuple-element.237), channel_id=1, source_target_pairs={{0,8},{1,9},{2,10},{3,11},{4,12},{5,13},{6,14},{7,15},{8,0},{9,1},... | collective-permute-start | bytes 417800 | tf_op jit(solution)/shard_map/ppermute | solution.py:143
  301.3 12.9 %collective-permute-start.42 = (bf16[4,136,128]{2,1,0:T(8,128)(2,1)S(1)}, bf16[4,136,128]{2,1,0:T(8,128)(2,1)S(1)}, u32[]{:S(2)}, u32[]{:S(2)}) collective-permute-start(bf16[4,136,128]{2,1,0:T(8,128)(2,1)S(1)} %get-tuple-element.239), channel_id=1, source_target_pairs={{0,8},{1,9},{2,10},{3,11},{4,12},{5,13},{6,14},{7,15},{8,0},{9,1},... | collective-permute-start | bytes 417800 | tf_op jit(solution)/shard_map/ppermute | solution.py:143
  303.4 16.6 %collective-permute-start.52 = (bf16[4,152,128]{2,1,0:T(8,128)(2,1)S(1)}, bf16[4,152,128]{2,1,0:T(8,128)(2,1)S(1)}, u32[]{:S(2)}, u32[]{:S(2)}) collective-permute-start(bf16[4,152,128]{2,1,0:T(8,128)(2,1)S(1)} %get-tuple-element.229), channel_id=1, source_target_pairs={{0,2},{1,3},{2,0},{3,1},{4,6},{5,7},{6,4},{7,5},{8,10},{9,11},{10,... | collective-permute-start | bytes 466952 | tf_op jit(solution)/shard_map/ppermute | solution.py:143
  306.8 14.4 %collective-permute-start.47 = (bf16[4,152,128]{2,1,0:T(8,128)(2,1)S(1)}, bf16[4,152,128]{2,1,0:T(8,128)(2,1)S(1)}, u32[]{:S(2)}, u32[]{:S(2)}) collective-permute-start(bf16[4,152,128]{2,1,0:T(8,128)(2,1)S(1)} %get-tuple-element.231), channel_id=1, source_target_pairs={{0,4},{1,5},{2,6},{3,7},{4,0},{5,1},{6,2},{7,3},{8,12},{9,13},{10,... | collective-permute-start | bytes 466952 | tf_op jit(solution)/shard_map/ppermute | solution.py:143
  310.0 13.0 %collective-permute-start.37 = (bf16[4,152,128]{2,1,0:T(8,128)(2,1)S(1)}, bf16[4,152,128]{2,1,0:T(8,128)(2,1)S(1)}, u32[]{:S(2)}, u32[]{:S(2)}) collective-permute-start(bf16[4,152,128]{2,1,0:T(8,128)(2,1)S(1)} %get-tuple-element.233), channel_id=1, source_target_pairs={{0,2},{1,3},{2,0},{3,1},{4,6},{5,7},{6,4},{7,5},{8,10},{9,11},{10,... | collective-permute-start | bytes 466952 | tf_op jit(solution)/shard_map/ppermute | solution.py:143
  312.1 11.5 %collective-permute-start.32 = (bf16[4,152,128]{2,1,0:T(8,128)(2,1)S(1)}, bf16[4,152,128]{2,1,0:T(8,128)(2,1)S(1)}, u32[]{:S(2)}, u32[]{:S(2)}) collective-permute-start(bf16[4,152,128]{2,1,0:T(8,128)(2,1)S(1)} %get-tuple-element.235), channel_id=1, source_target_pairs={{0,4},{1,5},{2,6},{3,7},{4,0},{5,1},{6,2},{7,3},{8,12},{9,13},{10,... | collective-permute-start | bytes 466952 | tf_op jit(solution)/shard_map/ppermute | solution.py:143
  318.6 16.3 %collective-permute-start.43 = (bf16[2,136,128]{2,1,0:T(8,128)(2,1)S(1)}, bf16[2,136,128]{2,1,0:T(8,128)(2,1)S(1)}, u32[]{:S(2)}, u32[]{:S(2)}) collective-permute-start(bf16[2,136,128]{2,1,0:T(8,128)(2,1)S(1)} %get-tuple-element.251), channel_id=1, source_target_pairs={{0,2},{1,3},{2,0},{3,1},{4,6},{5,7},{6,4},{7,5},{8,10},{9,11},{10,... | collective-permute-start | bytes 208904 | tf_op jit(solution)/shard_map/ppermute | solution.py:143
  319.9 16.0 %collective-permute-start.59 = (bf16[1,136,128]{2,1,0:T(8,128)(2,1)S(1)}, bf16[1,136,128]{2,1,0:T(8,128)(2,1)S(1)}, u32[]{:S(2)}, u32[]{:S(2)}) collective-permute-start(bf16[1,136,128]{2,1,0:T(8,128)(2,1)S(1)} %get-tuple-element.260), channel_id=1, source_target_pairs={{0,16},{1,17},{2,18},{3,19},{4,20},{5,21},{6,22},{7,23},{8,24},{9,... | collective-permute-start | bytes 104456 | tf_op jit(solution)/shard_map/ppermute | solution.py:143
  323.6 7.0 %collective-permute-start.38 = (bf16[2,152,128]{2,1,0:T(8,128)(2,1)S(1)}, bf16[2,152,128]{2,1,0:T(8,128)(2,1)S(1)}, u32[]{:S(2)}, u32[]{:S(2)}) collective-permute-start(bf16[2,152,128]{2,1,0:T(8,128)(2,1)S(1)} %get-tuple-element.245), channel_id=1, source_target_pairs={{0,4},{1,5},{2,6},{3,7},{4,0},{5,1},{6,2},{7,3},{8,12},{9,13},{10,... | collective-permute-start | bytes 233480 | tf_op jit(solution)/shard_map/ppermute | solution.py:143
  325.7 6.0 %collective-permute-start.33 = (bf16[2,152,128]{2,1,0:T(8,128)(2,1)S(1)}, bf16[2,152,128]{2,1,0:T(8,128)(2,1)S(1)}, u32[]{:S(2)}, u32[]{:S(2)}) collective-permute-start(bf16[2,152,128]{2,1,0:T(8,128)(2,1)S(1)} %get-tuple-element.247), channel_id=1, source_target_pairs={{0,8},{1,9},{2,10},{3,11},{4,12},{5,13},{6,14},{7,15},{8,0},{9,1},... | collective-permute-start | bytes 233480 | tf_op jit(solution)/shard_map/ppermute | solution.py:143
  327.5 23.6 %collective-permute-start.54 = (bf16[1,152,128]{2,1,0:T(8,128)(2,1)S(1)}, bf16[1,152,128]{2,1,0:T(8,128)(2,1)S(1)}, u32[]{:S(2)}, u32[]{:S(2)}) collective-permute-start(bf16[1,152,128]{2,1,0:T(8,128)(2,1)S(1)} %get-tuple-element.252), channel_id=1, source_target_pairs={{0,16},{1,17},{2,18},{3,19},{4,20},{5,21},{6,22},{7,23},{8,24},{9,... | collective-permute-start | bytes 116744 | tf_op jit(solution)/shard_map/ppermute | solution.py:143
  330.6 20.4 %collective-permute-start.49 = (bf16[1,152,128]{2,1,0:T(8,128)(2,1)S(1)}, bf16[1,152,128]{2,1,0:T(8,128)(2,1)S(1)}, u32[]{:S(2)}, u32[]{:S(2)}) collective-permute-start(bf16[1,152,128]{2,1,0:T(8,128)(2,1)S(1)} %get-tuple-element.254), channel_id=1, source_target_pairs={{0,16},{1,17},{2,18},{3,19},{4,20},{5,21},{6,22},{7,23},{8,24},{9,... | collective-permute-start | bytes 116744 | tf_op jit(solution)/shard_map/ppermute | solution.py:143
  331.7 19.4 %collective-permute-start.39 = (bf16[1,152,128]{2,1,0:T(8,128)(2,1)S(1)}, bf16[1,152,128]{2,1,0:T(8,128)(2,1)S(1)}, u32[]{:S(2)}, u32[]{:S(2)}) collective-permute-start(bf16[1,152,128]{2,1,0:T(8,128)(2,1)S(1)} %get-tuple-element.256), channel_id=1, source_target_pairs={{0,16},{1,17},{2,18},{3,19},{4,20},{5,21},{6,22},{7,23},{8,24},{9,... | collective-permute-start | bytes 116744 | tf_op jit(solution)/shard_map/ppermute | solution.py:143
  334.9 16.3 %collective-permute-start.34 = (bf16[1,152,128]{2,1,0:T(8,128)(2,1)S(1)}, bf16[1,152,128]{2,1,0:T(8,128)(2,1)S(1)}, u32[]{:S(2)}, u32[]{:S(2)}) collective-permute-start(bf16[1,152,128]{2,1,0:T(8,128)(2,1)S(1)} %get-tuple-element.258), channel_id=1, source_target_pairs={{0,16},{1,17},{2,18},{3,19},{4,20},{5,21},{6,22},{7,23},{8,24},{9,... | collective-permute-start | bytes 116744 | tf_op jit(solution)/shard_map/ppermute | solution.py:143
  335.9 15.2 %collective-permute-start.44 = (bf16[1,136,128]{2,1,0:T(8,128)(2,1)S(1)}, bf16[1,136,128]{2,1,0:T(8,128)(2,1)S(1)}, u32[]{:S(2)}, u32[]{:S(2)}) collective-permute-start(bf16[1,136,128]{2,1,0:T(8,128)(2,1)S(1)} %get-tuple-element.262), channel_id=1, source_target_pairs={{0,16},{1,17},{2,18},{3,19},{4,20},{5,21},{6,22},{7,23},{8,24},{9,... | collective-permute-start | bytes 104456 | tf_op jit(solution)/shard_map/ppermute | solution.py:143
  (51 other events, 657.3 us)
